TPU v7x, 256 devices: a whole 4x4x8 slice. The times are simulated.
256 devices in a mesh: row: 16 (over x, y_lo, core), span: 2 (over y_hi), pitch: 8 (over z).
Axes of the slice: x: 4, y: 4 (y_hi: 2, y_lo: 2; y = y_hi * 2 + y_lo), z: 8, core: 2. Of those that a mesh axis runs over, the one named last changes fastest.
Arguments:
- adjoint_start: float32 [5, 64, 64, 1024], P(None, 'row', 'span', 'pitch'), may hold values from -8 to 8
- source: float32 [5, 64, 64, 1024], P(None, 'row', 'span', 'pitch'), may hold values from -6 to 6
- couplings: float32 [6, 64, 64, 1024], P(None, 'row', 'span', 'pitch'), may hold values from 0.2 to 1
- damping: float32 [64, 64, 1024], P('row', 'span', 'pitch'), may hold values from 0.1 to 0.8
- jacobians: float32 [16, 6, 5, 5], P('row')
- giles_real: float32 [15, 64, 5, 5], replicated, may hold values from -6 to 6
- giles_imag: float32 [15, 64, 5, 5], replicated, may hold values from -6 to 6
- blades: int32 [16], replicated, may hold values from 16 to 79
- mode_orders: int32 [15, 64, 2], replicated, may hold values from -2 to 2
- cell_map: int32 [16, 1024], P('row'), may hold values from 0 to 1023
Outputs:
- adjoint: float32 [5, 64, 64, 1024], P(None, 'row', 'span', 'pitch')
All inputs are finite; a program needn't handle non-finite values.
Results may differ from a plain program's by a relative error of at most 0.0001.
Values sent between devices are 32-bit elements; how exact they have to be, the bound alone decides.
A program may use at most 64 MiB of HBM per device.

v0:
```python
import math

import jax
import jax.numpy as jnp
from jax import lax
from jax.sharding import PartitionSpec as P

ITERS = 5


PRECISE = lax.Precision.HIGHEST


def shifted(x, axis, by):
    size = lax.axis_size(axis)
    pairs = [(i, i + by) for i in range(size) if 0 <= i + by < size]
    return lax.ppermute(x, axis, pairs)


def padded(cells, sides, width, closed):
    for axis, dim in sides:
        count = lax.axis_size(axis)
        ends = count if closed else count - 1
        head = lax.slice_in_dim(cells, 0, width, axis=dim)
        tail = lax.slice_in_dim(cells, cells.shape[dim] - width, cells.shape[dim], axis=dim)
        cells = jnp.concatenate(
            [
                lax.ppermute(tail, axis, [(i, (i + 1) % count) for i in range(ends)]),
                cells,
                lax.ppermute(head, axis, [((i + 1) % count, i) for i in range(ends)]),
            ],
            axis=dim,
        )
    return cells


def phase_table(numbers, positions, length):
    products = positions[:, None] * numbers[None, :]
    return jnp.mod(products, length).astype(jnp.float32) * (2.0 * math.pi / length)


def giles(real_part, imag_part, giles_re, giles_im):
    out_real = jnp.einsum("kjc,jsk->csk", giles_re, real_part, precision=PRECISE) - jnp.einsum(
        "kjc,jsk->csk", giles_im, imag_part, precision=PRECISE
    )
    out_imag = jnp.einsum("kjc,jsk->csk", giles_re, imag_part, precision=PRECISE) + jnp.einsum(
        "kjc,jsk->csk", giles_im, real_part, precision=PRECISE
    )
    return jnp.stack([out_real, out_imag], 2)


def send_upstream(amplitudes):
    return shifted(amplitudes, "row", -1)


def update(adjoint, source, couplings, diag_sum, jacobian_row, boundary):
    axial_cells = adjoint.shape[1]
    span_len = adjoint.shape[2]
    pitch_len = adjoint.shape[3]
    span_edges = jnp.concatenate([adjoint[:, :, :1], adjoint[:, :, -1:]], 2)
    span_got = padded(span_edges, (("span", 2),), 1, False)
    pitch_edges = jnp.concatenate([adjoint[:, :, :, :1], adjoint[:, :, :, -1:]], 3)
    pitch_got = padded(pitch_edges, (("pitch", 3),), 1, True)
    axial_index = lax.broadcasted_iota(jnp.int32, (1, axial_cells, 1, 1), 1)
    span_index = lax.broadcasted_iota(jnp.int32, (1, 1, span_len, 1), 2)
    pitch_index = lax.broadcasted_iota(jnp.int32, (1, 1, 1, pitch_len), 3)
    axial_next = jnp.where(axial_index == axial_cells - 1, 0.0, jnp.roll(adjoint, -1, 1))
    axial_prev = jnp.where(axial_index == 0, 0.0, jnp.roll(adjoint, 1, 1))
    span_next = jnp.where(span_index == span_len - 1, span_got[:, :, 3:4], jnp.roll(adjoint, -1, 2))
    span_prev = jnp.where(span_index == 0, span_got[:, :, 0:1], jnp.roll(adjoint, 1, 2))
    pitch_next = jnp.where(
        pitch_index == pitch_len - 1, pitch_got[:, :, :, 3:4], jnp.roll(adjoint, -1, 3)
    )
    pitch_prev = jnp.where(pitch_index == 0, pitch_got[:, :, :, 0:1], jnp.roll(adjoint, 1, 3))
    neighbours = (axial_next, axial_prev, span_next, span_prev, pitch_next, pitch_prev)
    total = source + jnp.where(axial_index == axial_cells - 1, boundary[:, None], 0.0)
    for direction in range(6):
        mixed = jacobian_row[direction, 0][:, None, None, None] * neighbours[direction][0][None]
        for entry in range(1, 5):
            mixed = (
                mixed
                + jacobian_row[direction, entry][:, None, None, None]
                * neighbours[direction][entry][None]
            )
        total = total + couplings[direction][None] * mixed
    return total / diag_sum[None]


def on_device(
    adjoint_start,
    source,
    couplings,
    damping,
    jacobians,
    giles_real,
    giles_imag,
    blades,
    mode_orders,
    cell_map,
):
    components, axial_cells, span_cells, pitch_cells = adjoint_start.shape
    rows_all = lax.axis_size("row")
    pitch_count = lax.axis_size("pitch")
    span_count = lax.axis_size("span")
    length = pitch_cells * pitch_count
    modes_count = mode_orders.shape[1]
    row_id = lax.axis_index("row")
    diag_sum = damping + jnp.sum(couplings, 0)
    jacobian_row = jacobians[0]
    sender_face = jnp.maximum(row_id - 1, 0)
    receiver_face = jnp.minimum(row_id, rows_all - 2)

    def mode_numbers(face):
        orders = lax.dynamic_index_in_dim(mode_orders, face, 0, keepdims=False)
        blades_low = lax.dynamic_index_in_dim(blades, face, 0, keepdims=False)
        blades_high = lax.dynamic_index_in_dim(blades, face + 1, 0, keepdims=False)
        return orders[:, 0] * blades_low + orders[:, 1] * blades_high

    send_modes = mode_numbers(sender_face)
    recv_modes = mode_numbers(receiver_face)
    giles_re = lax.dynamic_index_in_dim(giles_real, sender_face, 0, keepdims=False)
    giles_im = lax.dynamic_index_in_dim(giles_imag, sender_face, 0, keepdims=False)
    donor_cells = cell_map[0]
    angles = phase_table(send_modes, jnp.arange(length, dtype=jnp.int32), length)
    whole_forward = jnp.concatenate([jnp.cos(angles), -jnp.sin(angles)], 1) * (2.0 / length)
    angles = phase_table(recv_modes, donor_cells, length)
    whole_synth = jnp.concatenate([jnp.cos(angles).T, -jnp.sin(angles).T], 0)
    adjoint = adjoint_start
    for sweep in range(ITERS):
        inlet_strip = adjoint[:, 0]
        transposed = lax.all_to_all(
            inlet_strip, ("span", "pitch"), split_axis=1, concat_axis=2, tiled=True
        )
        stations = transposed.shape[1] * span_count
        strip_rows = transposed.reshape(components * stations, length)
        coeffs = jnp.dot(strip_rows, whole_forward, precision=PRECISE).reshape(
            components, stations, 2, modes_count
        )
        treated = giles(coeffs[:, :, 0], coeffs[:, :, 1], giles_re, giles_im)
        arrived = send_upstream(treated)
        boundary_field = jnp.dot(
            arrived.reshape(components * stations, 2 * modes_count), whole_synth, precision=PRECISE
        )
        boundary_field = boundary_field.reshape(
            components, transposed.shape[1], span_count * length
        )
        boundary = lax.all_to_all(
            boundary_field, ("span", "pitch"), split_axis=2, concat_axis=1, tiled=True
        )
        adjoint = update(adjoint, source, couplings, diag_sum, jacobian_row, boundary)
    return adjoint


def solution(mesh):
    placed = (
        P(None, "row", "span", "pitch"),
        P(None, "row", "span", "pitch"),
        P(None, "row", "span", "pitch"),
        P("row", "span", "pitch"),
        P("row", None, None, None),
        P(),
        P(),
        P(),
        P(),
        P("row", None),
    )
    return jax.shard_map(
        on_device,
        mesh=mesh,
        in_specs=placed,
        out_specs=P(None, "row", "span", "pitch"),
        check_vma=False,
    )
```

profile of v0, /device:TPU:1, one launch (start us, length us, event | category | flops | bytes accessed | tf_op | source)
XLA Modules:
  0.0 459.5 jit_solution(9787683036794448431)
XLA Ops:
  1.7 11.7 %all-to-all-start = ((f32[5,32,128]{2,0,1:T(8,128)}), f32[5,32,128]{2,0,1:T(8,128)S(1)}, u32[]{:S(2)}, u32[]{:S(2)}) async-start(f32[5,32,128]{2,0,1:T(8,128)} %bitcast.421), calls=%async_computation | async-start | bytes 262144 | tf_op jit(solution)/shard_map/all_to_all | solution.py:131
  20.5 6.9 %collective-permute-start.2 = (f32[5,4,1,128]{3,0,2,1:T(8,128)S(1)}, f32[5,4,1,128]{3,0,2,1:T(8,128)}, u32[]{:S(2)}, u32[]{:S(2)}) collective-permute-start(f32[5,4,1,128]{3,0,2,1:T(8,128)S(1)} %copy.353), channel_id=1, source_target_pairs={{0,8},{1,9},{2,10},{3,11},{4,12},{5,13},{6,14},{7,15},{16,24},{17,... | collective-permute-start | bytes 30728 | tf_op jit(solution)/shard_map/ppermute | solution.py:28
  74.7 5.0 %reshape.216 = f32[16,1,1280]{2,1,0:T(1,128)} reshape(f32[2048,2,5]{2,1,0:T(2,128)} %bitcast.426) | data formatting | bytes 163840
  79.7 5.8 %all-to-all-start.1 = ((f32[16,1,1280]{2,1,0:T(1,128)}), f32[16,1,1280]{2,1,0:T(1,128)S(1)}, u32[]{:S(2)}, u32[]{:S(2)}) async-start(f32[16,1,1280]{2,1,0:T(1,128)} %reshape.216), calls=%async_computation.1 | async-start | bytes 163840 | tf_op jit(solution)/shard_map/all_to_all | solution.py:147
  86.4 7.9 %all-to-all-done.1 = f32[16,1,1280]{2,1,0:T(1,128)S(1)} async-done(((f32[16,1,1280]{2,1,0:T(1,128)}), f32[16,1,1280]{2,1,0:T(1,128)S(1)}, u32[]{:S(2)}, u32[]{:S(2)}) %all-to-all-start.1) | async-done | bytes 81952 | tf_op jit(solution)/shard_map/all_to_all | solution.py:147
  123.7 6.7 %collective-permute-start.7 = (f32[5,4,1,128]{3,0,2,1:T(8,128)S(1)}, f32[5,4,1,128]{3,0,2,1:T(8,128)}, u32[]{:S(2)}, u32[]{:S(2)}) collective-permute-start(f32[5,4,1,128]{3,0,2,1:T(8,128)S(1)} %get-tuple-element.187), channel_id=1, source_target_pairs={{0,8},{1,9},{2,10},{3,11},{4,12},{5,13},{6,14},{7,15},{16,24},{17,... | collective-permute-start | bytes 30728 | tf_op jit(solution)/shard_map/ppermute | solution.py:28
  135.7 7.4 %collective-permute-done.9 = f32[5,4,32,1]{3,0,2,1:T(8,128)} collective-permute-done((f32[5,4,32,1]{3,0,2,1:T(8,128)S(1)}, f32[5,4,32,1]{3,0,2,1:T(8,128)}, u32[]{:S(2)}, u32[]{:S(2)}) %collective-permute-start.9) | collective-permute-done | bytes 2592 | tf_op jit(solution)/shard_map/ppermute | solution.py:28
  153.0 4.9 %collective-permute-start.5 = (f32[5,4,2,64]{3,1,2,0:T(4,128)S(1)}, f32[5,4,2,64]{3,1,2,0:T(4,128)S(1)}, u32[]{:S(2)}, u32[]{:S(2)}) collective-permute-start(f32[5,4,2,64]{3,1,2,0:T(4,128)S(1)} %pad_maximum_fusion.7), channel_id=1, source_target_pairs={{16,0},{32,16},{48,32},{64,48},{80,64},{96,80},{112,96},{128,112},... | collective-permute-start | bytes 30728 | tf_op jit(solution)/shard_map/ppermute | solution.py:17
  164.1 5.0 %reshape.218 = f32[16,1,1280]{2,1,0:T(1,128)} reshape(f32[2048,2,5]{2,1,0:T(2,128)} %bitcast.428) | data formatting | bytes 163840
  174.6 7.9 %all-to-all-done.3 = f32[16,1,1280]{2,1,0:T(1,128)S(1)} async-done(((f32[16,1,1280]{2,1,0:T(1,128)}), f32[16,1,1280]{2,1,0:T(1,128)S(1)}, u32[]{:S(2)}, u32[]{:S(2)}) %all-to-all-start.3) | async-done | bytes 81952 | tf_op jit(solution)/shard_map/all_to_all | solution.py:147
  212.1 6.7 %collective-permute-start.12 = (f32[5,4,1,128]{3,0,2,1:T(8,128)S(1)}, f32[5,4,1,128]{3,0,2,1:T(8,128)}, u32[]{:S(2)}, u32[]{:S(2)}) collective-permute-start(f32[5,4,1,128]{3,0,2,1:T(8,128)S(1)} %get-tuple-element.144), channel_id=1, source_target_pairs={{0,8},{1,9},{2,10},{3,11},{4,12},{5,13},{6,14},{7,15},{16,24},{17,... | collective-permute-start | bytes 30728 | tf_op jit(solution)/shard_map/ppermute | solution.py:28
  225.8 7.6 %collective-permute-done.14 = f32[5,4,32,1]{3,0,2,1:T(8,128)} collective-permute-done((f32[5,4,32,1]{3,0,2,1:T(8,128)S(1)}, f32[5,4,32,1]{3,0,2,1:T(8,128)}, u32[]{:S(2)}, u32[]{:S(2)}) %collective-permute-start.14) | collective-permute-done | bytes 2592 | tf_op jit(solution)/shard_map/ppermute | solution.py:28
  252.0 5.0 %reshape.220 = f32[16,1,1280]{2,1,0:T(1,128)} reshape(f32[2048,2,5]{2,1,0:T(2,128)} %bitcast.430) | data formatting | bytes 163840
  257.0 4.8 %all-to-all-start.5 = ((f32[16,1,1280]{2,1,0:T(1,128)}), f32[16,1,1280]{2,1,0:T(1,128)S(1)}, u32[]{:S(2)}, u32[]{:S(2)}) async-start(f32[16,1,1280]{2,1,0:T(1,128)} %reshape.220), calls=%async_computation.5 | async-start | bytes 163840 | tf_op jit(solution)/shard_map/all_to_all | solution.py:147
  262.8 8.0 %all-to-all-done.5 = f32[16,1,1280]{2,1,0:T(1,128)S(1)} async-done(((f32[16,1,1280]{2,1,0:T(1,128)}), f32[16,1,1280]{2,1,0:T(1,128)S(1)}, u32[]{:S(2)}, u32[]{:S(2)}) %all-to-all-start.5) | async-done | bytes 81952 | tf_op jit(solution)/shard_map/all_to_all | solution.py:147
  300.3 6.7 %collective-permute-start.17 = (f32[5,4,1,128]{3,0,2,1:T(8,128)S(1)}, f32[5,4,1,128]{3,0,2,1:T(8,128)}, u32[]{:S(2)}, u32[]{:S(2)}) collective-permute-start(f32[5,4,1,128]{3,0,2,1:T(8,128)S(1)} %get-tuple-element.101), channel_id=1, source_target_pairs={{0,8},{1,9},{2,10},{3,11},{4,12},{5,13},{6,14},{7,15},{16,24},{17,... | collective-permute-start | bytes 30728 | tf_op jit(solution)/shard_map/ppermute | solution.py:28
  313.5 7.4 %collective-permute-done.19 = f32[5,4,32,1]{3,0,2,1:T(8,128)} collective-permute-done((f32[5,4,32,1]{3,0,2,1:T(8,128)S(1)}, f32[5,4,32,1]{3,0,2,1:T(8,128)}, u32[]{:S(2)}, u32[]{:S(2)}) %collective-permute-start.19) | collective-permute-done | bytes 2592 | tf_op jit(solution)/shard_map/ppermute | solution.py:28
  340.1 5.0 %reshape.222 = f32[16,1,1280]{2,1,0:T(1,128)} reshape(f32[2048,2,5]{2,1,0:T(2,128)} %bitcast.432) | data formatting | bytes 163840
  350.6 8.0 %all-to-all-done.7 = f32[16,1,1280]{2,1,0:T(1,128)S(1)} async-done(((f32[16,1,1280]{2,1,0:T(1,128)}), f32[16,1,1280]{2,1,0:T(1,128)S(1)}, u32[]{:S(2)}, u32[]{:S(2)}) %all-to-all-start.7) | async-done | bytes 81952 | tf_op jit(solution)/shard_map/all_to_all | solution.py:147
  388.2 6.7 %collective-permute-start.22 = (f32[5,4,1,128]{3,0,2,1:T(8,128)S(1)}, f32[5,4,1,128]{3,0,2,1:T(8,128)}, u32[]{:S(2)}, u32[]{:S(2)}) collective-permute-start(f32[5,4,1,128]{3,0,2,1:T(8,128)S(1)} %get-tuple-element.58), channel_id=1, source_target_pairs={{0,8},{1,9},{2,10},{3,11},{4,12},{5,13},{6,14},{7,15},{16,24},{17,... | collective-permute-start | bytes 30728 | tf_op jit(solution)/shard_map/ppermute | solution.py:28
  401.4 7.5 %collective-permute-done.24 = f32[5,4,32,1]{3,0,2,1:T(8,128)} collective-permute-done((f32[5,4,32,1]{3,0,2,1:T(8,128)S(1)}, f32[5,4,32,1]{3,0,2,1:T(8,128)}, u32[]{:S(2)}, u32[]{:S(2)}) %collective-permute-start.24) | collective-permute-done | bytes 2592 | tf_op jit(solution)/shard_map/ppermute | solution.py:28
  427.4 5.0 %reshape.224 = f32[16,1,1280]{2,1,0:T(1,128)} reshape(f32[2048,2,5]{2,1,0:T(2,128)} %bitcast.434) | data formatting | bytes 163840
  432.4 4.6 %all-to-all-start.9 = ((f32[16,1,1280]{2,1,0:T(1,128)}), f32[16,1,1280]{2,1,0:T(1,128)S(1)}, u32[]{:S(2)}, u32[]{:S(2)}) async-start(f32[16,1,1280]{2,1,0:T(1,128)} %reshape.224), calls=%async_computation.9 | async-start | bytes 163840 | tf_op jit(solution)/shard_map/all_to_all | solution.py:147
  437.3 8.7 %all-to-all-done.9 = f32[16,1,1280]{2,1,0:T(1,128)S(1)} async-done(((f32[16,1,1280]{2,1,0:T(1,128)}), f32[16,1,1280]{2,1,0:T(1,128)S(1)}, u32[]{:S(2)}, u32[]{:S(2)}) %all-to-all-start.9) | async-done | bytes 81952 | tf_op jit(solution)/shard_map/all_to_all | solution.py:147
  (564 shorter events, 295.3 us)
Async XLA Ops:
  1.7 60.9 %all-to-all-start = ((f32[5,32,128]{2,0,1:T(8,128)}), f32[5,32,128]{2,0,1:T(8,128)S(1)}, u32[]{:S(2)}, u32[]{:S(2)}) async-start(f32[5,32,128]{2,0,1:T(8,128)} %bitcast.421), calls=%async_computation | async-start | bytes 262144 | tf_op jit(solution)/shard_map/all_to_all | solution.py:131
  15.7 37.5 %collective-permute-start.3 = (f32[5,4,32,1]{3,0,2,1:T(8,128)}, f32[5,4,32,1]{3,0,2,1:T(8,128)}, u32[]{:S(2)}, u32[]{:S(2)}) collective-permute-start(f32[5,4,32,1]{3,0,2,1:T(8,128)} %copy.355), channel_id=1, source_target_pairs={{1,0},{2,1},{3,2},{4,3},{5,4},{6,5},{7,6},{0,7},{9,8},{10,9},{11,1... | collective-permute-start | bytes 7688 | tf_op jit(solution)/shard_map/ppermute | solution.py:30
  18.5 38.6 %collective-permute-start.4 = (f32[5,4,32,1]{3,0,2,1:T(8,128)S(1)}, f32[5,4,32,1]{3,0,2,1:T(8,128)}, u32[]{:S(2)}, u32[]{:S(2)}) collective-permute-start(f32[5,4,32,1]{3,0,2,1:T(8,128)S(1)} %copy.357), channel_id=1, source_target_pairs={{0,1},{1,2},{2,3},{3,4},{4,5},{5,6},{6,7},{7,0},{8,9},{9,10},{10,1... | collective-permute-start | bytes 7688 | tf_op jit(solution)/shard_map/ppermute | solution.py:28
  19.2 41.6 %collective-permute-start.1 = (f32[5,4,1,128]{3,0,2,1:T(8,128)}, f32[5,4,1,128]{3,0,2,1:T(8,128)}, u32[]{:S(2)}, u32[]{:S(2)}) collective-permute-start(f32[5,4,1,128]{3,0,2,1:T(8,128)} %copy.351), channel_id=1, source_target_pairs={{8,0},{9,1},{10,2},{11,3},{12,4},{13,5},{14,6},{15,7},{24,16},{25,... | collective-permute-start | bytes 30728 | tf_op jit(solution)/shard_map/ppermute | solution.py:30
  20.5 50.1 %collective-permute-start.2 = (f32[5,4,1,128]{3,0,2,1:T(8,128)S(1)}, f32[5,4,1,128]{3,0,2,1:T(8,128)}, u32[]{:S(2)}, u32[]{:S(2)}) collective-permute-start(f32[5,4,1,128]{3,0,2,1:T(8,128)S(1)} %copy.353), channel_id=1, source_target_pairs={{0,8},{1,9},{2,10},{3,11},{4,12},{5,13},{6,14},{7,15},{16,24},{17,... | collective-permute-start | bytes 30728 | tf_op jit(solution)/shard_map/ppermute | solution.py:28
  79.7 14.7 %all-to-all-start.1 = ((f32[16,1,1280]{2,1,0:T(1,128)}), f32[16,1,1280]{2,1,0:T(1,128)S(1)}, u32[]{:S(2)}, u32[]{:S(2)}) async-start(f32[16,1,1280]{2,1,0:T(1,128)} %reshape.216), calls=%async_computation.1 | async-start | bytes 163840 | tf_op jit(solution)/shard_map/all_to_all | solution.py:147
  111.5 37.8 %all-to-all-start.2 = ((f32[5,32,128]{2,0,1:T(8,128)}), f32[5,32,128]{2,0,1:T(8,128)S(1)}, u32[]{:S(2)}, u32[]{:S(2)}) async-start(f32[5,32,128]{2,0,1:T(8,128)} %get-tuple-element.164), calls=%async_computation.2 | async-start | bytes 262144 | tf_op jit(solution)/shard_map/all_to_all | solution.py:131
  122.4 25.1 %collective-permute-start.6 = (f32[5,4,1,128]{3,0,2,1:T(8,128)}, f32[5,4,1,128]{3,0,2,1:T(8,128)}, u32[]{:S(2)}, u32[]{:S(2)}) collective-permute-start(f32[5,4,1,128]{3,0,2,1:T(8,128)} %get-tuple-element.186), channel_id=1, source_target_pairs={{8,0},{9,1},{10,2},{11,3},{12,4},{13,5},{14,6},{15,7},{24,16},{25,... | collective-permute-start | bytes 30728 | tf_op jit(solution)/shard_map/ppermute | solution.py:30
  123.7 34.2 %collective-permute-start.7 = (f32[5,4,1,128]{3,0,2,1:T(8,128)S(1)}, f32[5,4,1,128]{3,0,2,1:T(8,128)}, u32[]{:S(2)}, u32[]{:S(2)}) collective-permute-start(f32[5,4,1,128]{3,0,2,1:T(8,128)S(1)} %get-tuple-element.187), channel_id=1, source_target_pairs={{0,8},{1,9},{2,10},{3,11},{4,12},{5,13},{6,14},{7,15},{16,24},{17,... | collective-permute-start | bytes 30728 | tf_op jit(solution)/shard_map/ppermute | solution.py:28
  199.9 39.7 %all-to-all-start.4 = ((f32[5,32,128]{2,0,1:T(8,128)}), f32[5,32,128]{2,0,1:T(8,128)S(1)}, u32[]{:S(2)}, u32[]{:S(2)}) async-start(f32[5,32,128]{2,0,1:T(8,128)} %get-tuple-element.121), calls=%async_computation.4 | async-start | bytes 262144 | tf_op jit(solution)/shard_map/all_to_all | solution.py:131
  207.7 14.2 %collective-permute-start.13 = (f32[5,4,32,1]{3,0,2,1:T(8,128)S(1)}, f32[5,4,32,1]{3,0,2,1:T(8,128)}, u32[]{:S(2)}, u32[]{:S(2)}) collective-permute-start(f32[5,4,32,1]{3,0,2,1:T(8,128)S(1)} %copy-done.4), channel_id=1, source_target_pairs={{1,0},{2,1},{3,2},{4,3},{5,4},{6,5},{7,6},{0,7},{9,8},{10,9},{11,1... | collective-permute-start | bytes 7688 | tf_op jit(solution)/shard_map/ppermute | solution.py:30
  210.8 26.9 %collective-permute-start.11 = (f32[5,4,1,128]{3,0,2,1:T(8,128)}, f32[5,4,1,128]{3,0,2,1:T(8,128)}, u32[]{:S(2)}, u32[]{:S(2)}) collective-permute-start(f32[5,4,1,128]{3,0,2,1:T(8,128)} %get-tuple-element.143), channel_id=1, source_target_pairs={{8,0},{9,1},{10,2},{11,3},{12,4},{13,5},{14,6},{15,7},{24,16},{25,... | collective-permute-start | bytes 30728 | tf_op jit(solution)/shard_map/ppermute | solution.py:30
  212.1 34.3 %collective-permute-start.12 = (f32[5,4,1,128]{3,0,2,1:T(8,128)S(1)}, f32[5,4,1,128]{3,0,2,1:T(8,128)}, u32[]{:S(2)}, u32[]{:S(2)}) collective-permute-start(f32[5,4,1,128]{3,0,2,1:T(8,128)S(1)} %get-tuple-element.144), channel_id=1, source_target_pairs={{0,8},{1,9},{2,10},{3,11},{4,12},{5,13},{6,14},{7,15},{16,24},{17,... | collective-permute-start | bytes 30728 | tf_op jit(solution)/shard_map/ppermute | solution.py:28
  218.8 14.6 %collective-permute-start.14 = (f32[5,4,32,1]{3,0,2,1:T(8,128)S(1)}, f32[5,4,32,1]{3,0,2,1:T(8,128)}, u32[]{:S(2)}, u32[]{:S(2)}) collective-permute-start(f32[5,4,32,1]{3,0,2,1:T(8,128)S(1)} %get-tuple-element.158), channel_id=1, source_target_pairs={{0,1},{1,2},{2,3},{3,4},{4,5},{5,6},{6,7},{7,0},{8,9},{9,10},{10,1... | collective-permute-start | bytes 7688 | tf_op jit(solution)/shard_map/ppermute | solution.py:28
  257.0 13.7 %all-to-all-start.5 = ((f32[16,1,1280]{2,1,0:T(1,128)}), f32[16,1,1280]{2,1,0:T(1,128)S(1)}, u32[]{:S(2)}, u32[]{:S(2)}) async-start(f32[16,1,1280]{2,1,0:T(1,128)} %reshape.220), calls=%async_computation.5 | async-start | bytes 163840 | tf_op jit(solution)/shard_map/all_to_all | solution.py:147
  288.1 39.0 %all-to-all-start.6 = ((f32[5,32,128]{2,0,1:T(8,128)}), f32[5,32,128]{2,0,1:T(8,128)S(1)}, u32[]{:S(2)}, u32[]{:S(2)}) async-start(f32[5,32,128]{2,0,1:T(8,128)} %get-tuple-element.78), calls=%async_computation.6 | async-start | bytes 262144 | tf_op jit(solution)/shard_map/all_to_all | solution.py:131
  296.0 13.7 %collective-permute-start.18 = (f32[5,4,32,1]{3,0,2,1:T(8,128)S(1)}, f32[5,4,32,1]{3,0,2,1:T(8,128)}, u32[]{:S(2)}, u32[]{:S(2)}) collective-permute-start(f32[5,4,32,1]{3,0,2,1:T(8,128)S(1)} %copy-done.5), channel_id=1, source_target_pairs={{1,0},{2,1},{3,2},{4,3},{5,4},{6,5},{7,6},{0,7},{9,8},{10,9},{11,1... | collective-permute-start | bytes 7688 | tf_op jit(solution)/shard_map/ppermute | solution.py:30
  299.0 26.3 %collective-permute-start.16 = (f32[5,4,1,128]{3,0,2,1:T(8,128)}, f32[5,4,1,128]{3,0,2,1:T(8,128)}, u32[]{:S(2)}, u32[]{:S(2)}) collective-permute-start(f32[5,4,1,128]{3,0,2,1:T(8,128)} %get-tuple-element.100), channel_id=1, source_target_pairs={{8,0},{9,1},{10,2},{11,3},{12,4},{13,5},{14,6},{15,7},{24,16},{25,... | collective-permute-start | bytes 30728 | tf_op jit(solution)/shard_map/ppermute | solution.py:30
  300.3 34.2 %collective-permute-start.17 = (f32[5,4,1,128]{3,0,2,1:T(8,128)S(1)}, f32[5,4,1,128]{3,0,2,1:T(8,128)}, u32[]{:S(2)}, u32[]{:S(2)}) collective-permute-start(f32[5,4,1,128]{3,0,2,1:T(8,128)S(1)} %get-tuple-element.101), channel_id=1, source_target_pairs={{0,8},{1,9},{2,10},{3,11},{4,12},{5,13},{6,14},{7,15},{16,24},{17,... | collective-permute-start | bytes 30728 | tf_op jit(solution)/shard_map/ppermute | solution.py:28
  307.0 13.9 %collective-permute-start.19 = (f32[5,4,32,1]{3,0,2,1:T(8,128)S(1)}, f32[5,4,32,1]{3,0,2,1:T(8,128)}, u32[]{:S(2)}, u32[]{:S(2)}) collective-permute-start(f32[5,4,32,1]{3,0,2,1:T(8,128)S(1)} %get-tuple-element.115), channel_id=1, source_target_pairs={{0,1},{1,2},{2,3},{3,4},{4,5},{5,6},{6,7},{7,0},{8,9},{9,10},{10,1... | collective-permute-start | bytes 7688 | tf_op jit(solution)/shard_map/ppermute | solution.py:28
  376.0 38.4 %all-to-all-start.8 = ((f32[5,32,128]{2,0,1:T(8,128)}), f32[5,32,128]{2,0,1:T(8,128)S(1)}, u32[]{:S(2)}, u32[]{:S(2)}) async-start(f32[5,32,128]{2,0,1:T(8,128)} %get-tuple-element.35), calls=%async_computation.8 | async-start | bytes 262144 | tf_op jit(solution)/shard_map/all_to_all | solution.py:131
  387.0 25.6 %collective-permute-start.21 = (f32[5,4,1,128]{3,0,2,1:T(8,128)}, f32[5,4,1,128]{3,0,2,1:T(8,128)}, u32[]{:S(2)}, u32[]{:S(2)}) collective-permute-start(f32[5,4,1,128]{3,0,2,1:T(8,128)} %get-tuple-element.57), channel_id=1, source_target_pairs={{8,0},{9,1},{10,2},{11,3},{12,4},{13,5},{14,6},{15,7},{24,16},{25,... | collective-permute-start | bytes 30728 | tf_op jit(solution)/shard_map/ppermute | solution.py:30
  388.2 33.6 %collective-permute-start.22 = (f32[5,4,1,128]{3,0,2,1:T(8,128)S(1)}, f32[5,4,1,128]{3,0,2,1:T(8,128)}, u32[]{:S(2)}, u32[]{:S(2)}) collective-permute-start(f32[5,4,1,128]{3,0,2,1:T(8,128)S(1)} %get-tuple-element.58), channel_id=1, source_target_pairs={{0,8},{1,9},{2,10},{3,11},{4,12},{5,13},{6,14},{7,15},{16,24},{17,... | collective-permute-start | bytes 30728 | tf_op jit(solution)/shard_map/ppermute | solution.py:28
  394.9 14.0 %collective-permute-start.24 = (f32[5,4,32,1]{3,0,2,1:T(8,128)S(1)}, f32[5,4,32,1]{3,0,2,1:T(8,128)}, u32[]{:S(2)}, u32[]{:S(2)}) collective-permute-start(f32[5,4,32,1]{3,0,2,1:T(8,128)S(1)} %get-tuple-element.72), channel_id=1, source_target_pairs={{0,1},{1,2},{2,3},{3,4},{4,5},{5,6},{6,7},{7,0},{8,9},{9,10},{10,1... | collective-permute-start | bytes 7688 | tf_op jit(solution)/shard_map/ppermute | solution.py:28
  (139 other events, 1108.0 us)
where the time goes:
time: 466 us; the launch traced here: 459 us
  local copies, waits for them, and re-layouts  162 us (35%)
  starting transfers between devices  124 us (27%)
  waiting for transfers between devices  87.8 us (19%)
  other arithmetic  66.2 us (14%)
  matrix products  16.6 us (4%)
    unnamed x280, local copies, waits for them, and re-layouts  57.3 us
    all_to_all x5, waiting for transfers between devices, on_device(): lax.all_to_all(boundary_field, ('span', 'pitch'), split_axis=2, concat_ax...  40.5 us
    ppermute x10, starting transfers between devices, padded(): lax.ppermute(tail, axis, [(i, (i + 1) % count) for i in range(ends)])  34.4 us
    ppermute x10, waiting for transfers between devices, padded(): lax.ppermute(tail, axis, [(i, (i + 1) % count) for i in range(ends)])  29.9 us
    slice x30, local copies, waits for them, and re-layouts, update(): neighbours[direction][0][None]  27.6 us
    all_to_all x5, starting transfers between devices, on_device(): lax.all_to_all(inlet_strip, ('span', 'pitch'), split_axis=1, concat_axis=...  25.8 us
    all_to_all x5, starting transfers between devices, on_device(): lax.all_to_all(boundary_field, ('span', 'pitch'), split_axis=2, concat_ax...  24.3 us
    ppermute x5, starting transfers between devices, shifted(): return lax.ppermute(x, axis, pairs)  20.3 us
  transfers between devices with their start and end apart: 35, of which 18 were waited for; matrix products, arithmetic and copies ran while one was open for 27% of the time, Pallas kernels for 0%

commit v1 on v0

v1 whole, which is shorter than its diff:
```python
import math

import jax
import jax.numpy as jnp
from jax import lax
from jax.experimental import pallas as pl
from jax.experimental.pallas import tpu as pltpu
from jax.sharding import PartitionSpec as P

ITERS = 5
MESH = pl.DeviceIdType.MESH
F32 = jnp.float32
BF16 = jnp.bfloat16
I32 = jnp.int32

ROUNDS = (
    (0, (0, 1, 2, 3)),
    (1, (0, 1, 2)),
    (2, (0, 1)),
    (3, (0,)),
    (1, (3,)),
    (2, (2, 3)),
    (3, (1, 2, 3)),
    (4, (0, 1, 2, 3)),
)
ROUND_OF = {(sweep, layer): i for i, (sweep, layers) in enumerate(ROUNDS) for layer in layers}


def sine(turns, length):
    half, quarter = length // 2, length // 4
    t = ((turns + half) & (length - 1)) - half
    t = jnp.where(t > quarter, half - t, jnp.where(t < -quarter, -half - t, t))
    x = t.astype(F32) * (2.0 * math.pi / length)
    y = x * x
    poly = 1.0 / 6227020800.0
    for c in (-1.0 / 39916800.0, 1.0 / 362880.0, -1.0 / 5040.0, 1.0 / 120.0, -1.0 / 6.0):
        poly = poly * y + c
    return x + x * (y * poly)


def split(x):
    high = x.astype(BF16)
    return high, (x - high.astype(F32)).astype(BF16)


def dot(a, b):
    return jnp.dot(a, b, preferred_element_type=F32)


def lane_modes(index, blades_low, blades_high):
    comp = (index * 41) >> 10
    u = index - 25 * comp
    mode = jnp.where(u >= 12, u, 24 - u)
    first = (mode * 13) >> 6
    second = mode - 5 * first
    return comp, u, mode, (first - 2) * blades_low + (second - 2) * blades_high


def kernel(
    rows,
    pitches,
    adj_hbm,
    src_hbm,
    cpl_hbm,
    dmp_hbm,
    jac,
    gr_hbm,
    gi_hbm,
    blades,
    ord_hbm,
    map_hbm,
    out_hbm,
    buf,
    src,
    cpl,
    dmp,
    gre,
    gim,
    orders,
    donors,
    gmix,
    fwd_hi,
    fwd_lo,
    syn_hi,
    syn_lo,
    coef_out,
    coef_in,
    right_out,
    left_out,
    from_left,
    from_right,
    edge_out,
    edge_in,
    load_sem,
    store_sem,
    coef_send,
    coef_recv,
    halo_send,
    halo_recv,
):
    row, span, pitch = lax.axis_index("row"), lax.axis_index("span"), lax.axis_index("pitch")
    length = 128 * pitches
    last = rows - 1
    right, left = lax.rem(pitch + 1, pitches), lax.rem(pitch + pitches - 1, pitches)
    face = jnp.minimum(row, rows - 2)
    sent_face = jnp.maximum(row - 1, 0)

    barrier = pltpu.get_barrier_semaphore()

    def greet(target):
        pl.semaphore_signal(barrier, inc=1, device_id=target, device_id_type=MESH)

    offsets = sorted(range(pitches), key=lambda o: -min(o, pitches - o))

    @pl.when(row > 0)
    def _():
        for o in offsets:
            greet({"row": row - 1, "pitch": lax.rem(pitch + o, pitches)})

    @pl.when(row < last)
    def _():
        for o in offsets:
            greet({"row": row + 1, "pitch": lax.rem(pitch + o, pitches)})

    greet({"span": 1 - span})
    greet({"pitch": right})
    greet({"pitch": left})

    loads = [
        pltpu.make_async_copy(adj_hbm, buf.at[0], load_sem.at[0]),
        pltpu.make_async_copy(cpl_hbm, cpl, load_sem.at[1]),
        pltpu.make_async_copy(dmp_hbm, dmp, load_sem.at[2]),
        pltpu.make_async_copy(src_hbm, src, load_sem.at[3]),
        pltpu.make_async_copy(ord_hbm.at[face], orders, load_sem.at[4]),
        pltpu.make_async_copy(
            map_hbm.at[:, pl.ds(pl.multiple_of(pitch * 128, 128), 128)], donors, load_sem.at[5]
        ),
        pltpu.make_async_copy(gr_hbm, gre, load_sem.at[6]),
        pltpu.make_async_copy(gi_hbm, gim, load_sem.at[7]),
    ]
    for copy in loads:
        copy.start()

    lane = lax.broadcasted_iota(I32, (32, 128), 1)
    srow = lax.broadcasted_iota(I32, (32, 128), 0)
    block = (lane * 41) >> 10

    wide_lane = lax.broadcasted_iota(I32, (128, 128), 1)
    wide_row = lax.broadcasted_iota(I32, (128, 128), 0)
    comp, u, mode, number = lane_modes(wide_lane, blades[sent_face], blades[sent_face + 1])
    turns = number * (wide_row + pitch * 128) + jnp.where(u >= 12, length // 4, length // 2)
    table = jnp.where(comp < 5, sine(turns, length) * (2.0 / length), 0.0)
    high, low = split(table)
    fwd_hi[...] = high
    fwd_lo[...] = low

    @pl.when(row == last)
    def _():
        coef_in[...] = jnp.zeros_like(coef_in)

    def coef_copy(n, target):
        return pltpu.make_async_remote_copy(
            src_ref=coef_out.at[n],
            dst_ref=coef_in.at[n, pitch],
            send_sem=coef_send.at[n, target],
            recv_sem=coef_recv.at[n, pitch],
            device_id={"row": jnp.maximum(row - 1, 0), "pitch": target},
            device_id_type=MESH,
        )

    def coef_arrival(n, sender):
        return pltpu.make_async_copy(coef_in.at[n, sender], coef_in.at[n, sender], coef_recv.at[n, sender])

    def project(n):
        strip = buf[n, :, 0].reshape(160, 128)
        high, low = split(strip)
        both = dot(high, fwd_hi[...]) + (dot(low, fwd_hi[...]) + dot(high, fwd_lo[...]))
        total = jnp.zeros((32, 128), F32)
        for c in range(5):
            total = total + jnp.where(block == c, both[32 * c : 32 * c + 32], 0.0)
        coef_out[n] = total

    def send_coefs(n):
        @pl.when(row > 0)
        def _():
            for o in offsets:
                coef_copy(n, lax.rem(pitch + o, pitches)).start()

    def halo_copies(i):
        return (
            pltpu.make_async_remote_copy(
                src_ref=right_out.at[i],
                dst_ref=from_left.at[i],
                send_sem=halo_send.at[i, 0],
                recv_sem=halo_recv.at[i, 0],
                device_id={"pitch": right},
                device_id_type=MESH,
            ),
            pltpu.make_async_remote_copy(
                src_ref=left_out.at[i],
                dst_ref=from_right.at[i],
                send_sem=halo_send.at[i, 1],
                recv_sem=halo_recv.at[i, 1],
                device_id={"pitch": left},
                device_id_type=MESH,
            ),
            pltpu.make_async_remote_copy(
                src_ref=edge_out.at[i],
                dst_ref=edge_in.at[i],
                send_sem=halo_send.at[i, 2],
                recv_sem=halo_recv.at[i, 2],
                device_id={"span": 1 - span},
                device_id_type=MESH,
            ),
        )

    def pack(i):
        n, layers = ROUNDS[i]
        to_right = jnp.zeros((32, 128), F32)
        to_left = jnp.zeros((32, 128), F32)
        for a in layers:
            for c in range(5):
                x = buf[n, c, a]
                at = 8 * a + c
                to_right = jnp.where(lane == at, pltpu.roll(x, at + 1, 1), to_right)
                to_left = jnp.where(lane == at, pltpu.roll(x, at, 1) if at else x, to_left)
                edge_out[i, at : at + 1, :] = jnp.where(span == 0, x[31:32], x[0:1])
        right_out[i] = to_right
        left_out[i] = to_left

    def send_halo(i):
        for copy in halo_copies(i):
            copy.start()

    def wait_halo(i):
        for copy in halo_copies(i):
            copy.wait_recv()

    def sweep_layer(n, a):
        i = ROUND_OF[n, a]
        total = [src[c, a] for c in range(5)]

        def add(direction, neighbours):
            weight = cpl[direction, a]
            for c in range(5):
                mixed = jac[0, c, 0, direction] * neighbours[0]
                for j in range(1, 5):
                    mixed = mixed + jac[j, c, 0, direction] * neighbours[j]
                total[c] = total[c] + weight * mixed

        if a < 3:
            add(0, [buf[n, j, a + 1] for j in range(5)])
        if a > 0:
            add(1, [buf[n, j, a - 1] for j in range(5)])
        cells = [buf[n, j, a] for j in range(5)]
        edges = [edge_in[i, 8 * a + j : 8 * a + j + 1, :] for j in range(5)]
        add(2, [jnp.where(srow == 31, edges[j], pltpu.roll(cells[j], 31, 0)) for j in range(5)])
        add(3, [jnp.where(srow == 0, edges[j], pltpu.roll(cells[j], 1, 0)) for j in range(5)])
        ends = [from_right[i, :, 8 * a + j : 8 * a + j + 1] for j in range(5)]
        add(4, [jnp.where(lane == 127, ends[j], pltpu.roll(cells[j], 127, 1)) for j in range(5)])
        ends = [from_left[i, :, 8 * a + j : 8 * a + j + 1] for j in range(5)]
        add(5, [jnp.where(lane == 0, ends[j], pltpu.roll(cells[j], 1, 1)) for j in range(5)])
        for c in range(5):
            buf[n + 1, c, a] = total[c]

    def add_boundary(n):
        @pl.when(row < last)
        def _():
            for o in range(pitches):
                coef_arrival(n, o).wait()

        coefs = coef_in[n, 0]
        for o in range(1, pitches):
            coefs = coefs + coef_in[n, o]
        high, low = split(coefs)
        field = dot(high, syn_hi[...]) + (dot(low, syn_hi[...]) + dot(high, syn_lo[...]))
        for c in range(5):
            buf[n + 1, c, 3] = buf[n + 1, c, 3] + field[:, 128 * c : 128 * c + 128] * dmp[3]

    loads[0].wait()
    project(0)
    pack(0)

    partners = 3 + pitches * ((row > 0).astype(I32) + (row < last).astype(I32))
    pl.semaphore_wait(barrier, partners)
    send_coefs(0)
    send_halo(0)

    for copy in loads[1:4]:
        copy.wait()
    keep_next = jnp.where((srow == 31) & (span == 1), 0.0, 1.0)
    keep_prev = jnp.where((srow == 0) & (span == 0), 0.0, 1.0)
    for a in range(4):
        diag = dmp[a]
        for d in range(6):
            diag = diag + cpl[d, a]
        inverse = 1.0 / diag
        dmp[a] = inverse
        for d in range(6):
            weight = cpl[d, a] * inverse
            if d == 2:
                weight = weight * keep_next
            if d == 3:
                weight = weight * keep_prev
            cpl[d, a] = weight
        for c in range(5):
            src[c, a] = src[c, a] * inverse

    for copy in loads[4:]:
        copy.wait()
    for j in range(5):
        for c in range(5):
            gmix[5 * j + c : 5 * j + c + 1, 0:64] = gre[j, c, pl.ds(face, 1), :]
            gmix[5 * j + c : 5 * j + c + 1, 64:128] = gim[j, c, pl.ds(face, 1), :]
    gmix[25:32, :] = jnp.zeros((7, 128), F32)
    one = (orders[0:1, :] + 2) * 5 + (orders[1:2, :] + 2)
    mode_of = jnp.concatenate([one, one], axis=1)
    comp, u, mode, number = lane_modes(wide_row, blades[face], blades[face + 1])
    same = jnp.where(mode_of == mode, 1.0, 0.0)
    opposite = jnp.where(mode_of == 24 - mode, 1.0, 0.0)
    either = jnp.maximum(same, opposite)
    signed = same - opposite
    in_real = wide_lane < 64
    cosine_row = u >= 12
    for_cos = jnp.where(
        cosine_row, jnp.where(in_real, either, 0.0), jnp.where(in_real, 0.0, -signed)
    )
    for_sin = jnp.where(
        cosine_row, jnp.where(in_real, 0.0, -signed), jnp.where(in_real, -either, 0.0)
    )
    contract = (((1,), (1,)), ((), ()))
    cos_mix = lax.dot_general(
        for_cos, gmix[...], contract, precision=lax.Precision.HIGHEST, preferred_element_type=F32
    )
    sin_mix = lax.dot_general(
        for_sin, gmix[...], contract, precision=lax.Precision.HIGHEST, preferred_element_type=F32
    )
    turns = number * donors[...]
    cosine = jnp.where(comp < 5, sine(turns + length // 4, length), 0.0)
    minus = jnp.where(comp < 5, sine(turns, length), 0.0)
    pick = lax.broadcasted_iota(I32, (128, 32), 1)
    pick_comp = (lax.broadcasted_iota(I32, (128, 32), 0) * 41) >> 10
    for c in range(5):
        chosen = pick == 5 * pick_comp + c
        on_cos = jnp.sum(jnp.where(chosen, cos_mix, 0.0), axis=1, keepdims=True)
        on_sin = jnp.sum(jnp.where(chosen, sin_mix, 0.0), axis=1, keepdims=True)
        high, low = split(on_cos * cosine + on_sin * minus)
        syn_hi[:, 128 * c : 128 * c + 128] = high
        syn_lo[:, 128 * c : 128 * c + 128] = low

    wait_halo(0)
    for a in (0, 1, 2):
        sweep_layer(0, a)
    pack(1)
    send_halo(1)
    project(1)
    send_coefs(1)
    sweep_layer(0, 3)
    wait_halo(1)
    sweep_layer(1, 0)
    sweep_layer(1, 1)
    pack(2)
    send_halo(2)
    project(2)
    send_coefs(2)
    wait_halo(2)
    sweep_layer(2, 0)
    pack(3)
    send_halo(3)
    project(3)
    send_coefs(3)

    add_boundary(0)
    pack(4)
    send_halo(4)
    sweep_layer(1, 2)
    sweep_layer(2, 1)
    wait_halo(3)
    sweep_layer(3, 0)
    project(4)
    send_coefs(4)

    wait_halo(4)
    sweep_layer(1, 3)
    add_boundary(1)
    pack(5)
    send_halo(5)
    wait_halo(5)
    sweep_layer(2, 2)
    sweep_layer(2, 3)
    add_boundary(2)
    pack(6)
    send_halo(6)
    wait_halo(6)
    for a in (1, 2, 3):
        sweep_layer(3, a)
    add_boundary(3)
    pack(7)
    send_halo(7)
    wait_halo(7)
    stores = []
    for a in range(4):
        sweep_layer(4, a)
        if a == 3:
            add_boundary(4)
        copy = pltpu.make_async_copy(buf.at[5, :, a], out_hbm.at[:, a], store_sem.at[a])
        copy.start()
        stores.append(copy)

    for i in range(len(ROUNDS)):
        for copy in halo_copies(i):
            copy.wait_send()

    @pl.when(row > 0)
    def _():
        for n in range(ITERS):
            for o in range(pitches):
                coef_copy(n, o).wait_send()

    for copy in stores:
        copy.wait()


def on_device(
    rows,
    pitches,
    adjoint_start,
    source,
    couplings,
    damping,
    jacobians,
    giles_real,
    giles_imag,
    blades,
    mode_orders,
    cell_map,
):
    faces = rows - 1
    rounds = len(ROUNDS)
    anywhere = pl.BlockSpec(memory_space=pl.ANY)
    scalars = pl.BlockSpec(memory_space=pltpu.SMEM)
    dma = pltpu.SemaphoreType.DMA
    scratch = [
        pltpu.VMEM((ITERS + 1, 5, 4, 32, 128), F32),
        pltpu.VMEM((5, 4, 32, 128), F32),
        pltpu.VMEM((6, 4, 32, 128), F32),
        pltpu.VMEM((4, 32, 128), F32),
        pltpu.VMEM((5, 5, faces, 64), F32),
        pltpu.VMEM((5, 5, faces, 64), F32),
        pltpu.VMEM((2, 64), I32),
        pltpu.VMEM((1, 128), I32),
        pltpu.VMEM((32, 128), F32),
        pltpu.VMEM((128, 128), BF16),
        pltpu.VMEM((128, 128), BF16),
        pltpu.VMEM((128, 640), BF16),
        pltpu.VMEM((128, 640), BF16),
        pltpu.VMEM((ITERS, 32, 128), F32),
        pltpu.VMEM((ITERS, pitches, 32, 128), F32),
        pltpu.VMEM((rounds, 32, 128), F32),
        pltpu.VMEM((rounds, 32, 128), F32),
        pltpu.VMEM((rounds, 32, 128), F32),
        pltpu.VMEM((rounds, 32, 128), F32),
        pltpu.VMEM((rounds, 32, 128), F32),
        pltpu.VMEM((rounds, 32, 128), F32),
        dma((8,)),
        dma((4,)),
        dma((ITERS, pitches)),
        dma((ITERS, pitches)),
        dma((rounds, 3)),
        dma((rounds, 3)),
    ]

    def body(*refs):
        kernel(rows, pitches, *refs)

    return pl.pallas_call(
        body,
        name="sweeps",
        out_shape=jax.ShapeDtypeStruct(adjoint_start.shape, F32),
        in_specs=[
            anywhere,
            anywhere,
            anywhere,
            anywhere,
            scalars,
            anywhere,
            anywhere,
            scalars,
            anywhere,
            anywhere,
        ],
        out_specs=anywhere,
        scratch_shapes=scratch,
        compiler_params=pltpu.CompilerParams(collective_id=0, has_side_effects=True),
    )(
        adjoint_start,
        source,
        couplings,
        damping,
        jnp.transpose(jacobians, (2, 3, 0, 1)),
        jnp.transpose(giles_real, (2, 3, 0, 1)),
        jnp.transpose(giles_imag, (2, 3, 0, 1)),
        blades,
        jnp.transpose(mode_orders, (0, 2, 1)),
        cell_map,
    )


def solution(mesh):
    rows, pitches = mesh.shape["row"], mesh.shape["pitch"]

    def step(*args):
        return on_device(rows, pitches, *args)

    placed = (
        P(None, "row", "span", "pitch"),
        P(None, "row", "span", "pitch"),
        P(None, "row", "span", "pitch"),
        P("row", "span", "pitch"),
        P("row", None, None, None),
        P(),
        P(),
        P(),
        P(),
        P("row", None),
    )
    return jax.shard_map(
        step,
        mesh=mesh,
        in_specs=placed,
        out_specs=P(None, "row", "span", "pitch"),
        check_vma=False,
    )
```

time: 466 us -> 49.8 us (0.11)
  the two profiles are of different devices: /device:TPU:1 before, /device:TPU:2 now
where the time goes in v1:
time: 49.8 us; the launch traced here: 49.6 us
  Pallas kernels  47.8 us (96%)
  local copies, waits for them, and re-layouts  1.72 us (3%)
    pallas_call x1, Pallas kernels, on_device(): pl.pallas_call(body, name='sweeps', out_shape=jax.ShapeDtypeStruct(adjoin...  47.8 us
    unnamed x1, local copies, waits for them, and re-layouts  1.72 us

profile of v1, /device:TPU:2, one launch (start us, length us, event | category | flops | bytes accessed | tf_op | source)
XLA Modules:
  0.0 49.6 jit_solution(2764517924159054540)
XLA Ops:
  0.0 47.8 %sweeps.1 = f32[5,4,32,128]{3,2,1,0:T(8,128)} custom-call(f32[5,4,32,128]{3,2,1,0:T(8,128)} %refs_0_.1, f32[5,4,32,128]{3,2,1,0:T(8,128)} %refs_1_.1, f32[6,4,32,128]{3,2,1,0:T(8,128)} %refs_2_.1, f32[4,32,128]{2,1,0:T(8,128)} %refs_3_.1, f32[5,5,1,6]{3,2,1,0:T(1,128)} %bitcast.7, f32[5,5,15,64]{3,2,1,0:T(8,128)} %bitcast.4, f32[5,5,15,64]{3,2,1,0:T(8,128)} %bitcast.5, ...), custom_call_target="tpu_custom_call" | custom-call | tf_op jit(solution)/shard_map/sweeps/pallas_call | solution.py:476
  47.8 1.7 %copy.12 = f32[5,4,32,128]{3,2,1,0:T(8,128)} copy(f32[5,4,32,128]{3,2,1,0:T(8,128)} %sweeps.1) | data formatting | bytes 655360

commit v2 on v1

v2 whole, which is shorter than its diff:
```python
import math

import jax
import jax.numpy as jnp
from jax import lax
from jax.experimental import pallas as pl
from jax.experimental.pallas import tpu as pltpu
from jax.sharding import PartitionSpec as P

ITERS = 5
MESH = pl.DeviceIdType.MESH
F32 = jnp.float32
BF16 = jnp.bfloat16
I32 = jnp.int32

def sine(turns, length):
    half, quarter = length // 2, length // 4
    t = ((turns + half) & (length - 1)) - half
    t = jnp.where(t > quarter, half - t, jnp.where(t < -quarter, -half - t, t))
    x = t.astype(F32) * (2.0 * math.pi / length)
    y = x * x
    poly = 1.0 / 6227020800.0
    for c in (-1.0 / 39916800.0, 1.0 / 362880.0, -1.0 / 5040.0, 1.0 / 120.0, -1.0 / 6.0):
        poly = poly * y + c
    return x + x * (y * poly)


def split(x):
    high = x.astype(BF16)
    return high, (x - high.astype(F32)).astype(BF16)


def dot(a, b):
    return jnp.dot(a, b, preferred_element_type=F32)


def lane_modes(index, blades_low, blades_high):
    comp = (index * 41) >> 10
    u = index - 25 * comp
    mode = jnp.where(u >= 12, u, 24 - u)
    first = (mode * 13) >> 6
    second = mode - 5 * first
    return comp, u, mode, (first - 2) * blades_low + (second - 2) * blades_high


def kernel(
    rows,
    pitches,
    adj_hbm,
    src_hbm,
    cpl_hbm,
    dmp_hbm,
    jac,
    gr_hbm,
    gi_hbm,
    blades,
    ord_hbm,
    map_hbm,
    out_hbm,
    buf,
    src,
    cpl,
    inv,
    src_raw,
    cpl_raw,
    dmp_raw,
    result,
    gre,
    gim,
    orders,
    donors,
    gmix,
    fwd_hi,
    fwd_lo,
    syn_hi,
    syn_lo,
    coef_out,
    coef_in,
    right_out,
    left_out,
    from_left,
    from_right,
    load_sem,
    store_sem,
    coef_send,
    coef_recv,
    halo_send,
    halo_recv,
):
    row, span, pitch = lax.axis_index("row"), lax.axis_index("span"), lax.axis_index("pitch")
    length = 128 * pitches
    last = rows - 1
    right, left = lax.rem(pitch + 1, pitches), lax.rem(pitch + pitches - 1, pitches)
    face = jnp.minimum(row, rows - 2)
    upstream = jnp.maximum(row - 1, 0)
    other = 1 - span
    edge = pl.ds(pl.multiple_of(24 * other, 8), 8)

    barrier = pltpu.get_barrier_semaphore()

    def greet(target):
        pl.semaphore_signal(barrier, inc=1, device_id=target, device_id_type=MESH)

    offsets = sorted(range(pitches), key=lambda o: -min(o, pitches - o))

    def partners_of(there):
        for o in offsets:
            for half in (span, other):
                greet({"row": there, "span": half, "pitch": lax.rem(pitch + o, pitches)})

    @pl.when(row > 0)
    def _():
        partners_of(row - 1)

    @pl.when(row < last)
    def _():
        partners_of(row + 1)

    greet({"span": other})
    for side in (right, left):
        greet({"pitch": side})
        greet({"span": other, "pitch": side})

    def donor_load(slot, where):
        cells = pl.ds(pl.multiple_of(where * 128, 128), 128)
        return pltpu.make_async_copy(map_hbm.at[:, cells], donors.at[slot], load_sem.at[7 + slot])

    loads = [
        pltpu.make_async_copy(adj_hbm, buf.at[0, 0, :, :, 0:32, :], load_sem.at[0]),
        pltpu.make_async_copy(cpl_hbm, cpl_raw, load_sem.at[1]),
        pltpu.make_async_copy(dmp_hbm, dmp_raw, load_sem.at[2]),
        pltpu.make_async_copy(src_hbm, src_raw, load_sem.at[3]),
        pltpu.make_async_copy(ord_hbm.at[face], orders, load_sem.at[4]),
        pltpu.make_async_copy(gr_hbm, gre, load_sem.at[5]),
        pltpu.make_async_copy(gi_hbm, gim, load_sem.at[6]),
        donor_load(0, pitch),
        donor_load(1, right),
        donor_load(2, left),
    ]
    for copy in loads:
        copy.start()

    lane = lax.broadcasted_iota(I32, (32, 128), 1)
    long_lane = lax.broadcasted_iota(I32, (40, 128), 1)
    srow = lax.broadcasted_iota(I32, (32, 128), 0)
    block = (lane * 41) >> 10

    wide_lane = lax.broadcasted_iota(I32, (128, 128), 1)
    wide_row = lax.broadcasted_iota(I32, (128, 128), 0)
    comp, u, mode, number = lane_modes(wide_lane, blades[upstream], blades[upstream + 1])
    turns = number * (wide_row + pitch * 128) + jnp.where(u >= 12, length // 4, length // 2)
    table = jnp.where(comp < 5, sine(turns, length) * (2.0 / length), 0.0)
    high, low = split(table)
    fwd_hi[...] = high
    fwd_lo[...] = low

    @pl.when(row == last)
    def _():
        coef_in[...] = jnp.zeros_like(coef_in)

    def coef_copy(n, part, target):
        source = coef_out.at[n, edge] if part else coef_out.at[n]
        landing = pl.ds(32, 8) if part else pl.ds(0, 32)
        return pltpu.make_async_remote_copy(
            src_ref=source,
            dst_ref=coef_in.at[n, pitch, landing],
            send_sem=coef_send.at[n, part, target],
            recv_sem=coef_recv.at[n, part, pitch],
            device_id={"row": upstream, "span": other if part else span, "pitch": target},
            device_id_type=MESH,
        )

    def coef_arrival(n, part, sender):
        landing = pl.ds(32, 8) if part else pl.ds(0, 32)
        there = coef_in.at[n, sender, landing]
        return pltpu.make_async_copy(there, there, coef_recv.at[n, part, sender])

    def parts_of(n):
        return (0, 1) if n < ITERS - 1 else (0,)

    def project(n):
        strip = buf[n, 0, :, 0, 0:32, :].reshape(160, 128)
        high, low = split(strip)
        both = dot(high, fwd_hi[...]) + (dot(low, fwd_hi[...]) + dot(high, fwd_lo[...]))
        total = jnp.zeros((32, 128), F32)
        for c in range(5):
            total = total + jnp.where(block == c, both[32 * c : 32 * c + 32], 0.0)
        coef_out[n] = total

    def send_coefs(n):
        @pl.when(row > 0)
        def _():
            for part in parts_of(n):
                for o in offsets:
                    coef_copy(n, part, lax.rem(pitch + o, pitches)).start()

    def wait_coefs(n):
        @pl.when(row < last)
        def _():
            for part in parts_of(n):
                for o in range(pitches):
                    coef_arrival(n, part, o).wait()

    def halo_copy(i, source, landing, target):
        return pltpu.make_async_remote_copy(
            src_ref=source,
            dst_ref=landing,
            send_sem=halo_send.at[i],
            recv_sem=halo_recv.at[i],
            device_id=target,
            device_id_type=MESH,
        )

    side_halos = [
        halo_copy(0, right_out, from_left.at[:, 0:32, :], {"pitch": right}),
        halo_copy(1, left_out, from_right.at[:, 0:32, :], {"pitch": left}),
        halo_copy(2, right_out.at[:, edge, :], from_left.at[:, 32:40, :], {"span": other, "pitch": right}),
        halo_copy(3, left_out.at[:, edge, :], from_right.at[:, 32:40, :], {"span": other, "pitch": left}),
    ]
    start_halo = halo_copy(
        4, buf.at[0, 0, :, :, edge, :], buf.at[0, 0, :, :, 32:40, :], {"span": other}
    )
    layer_halos = [
        (
            halo_copy(5 + a, cpl.at[0, :, a, edge, :], cpl.at[0, :, a, 32:40, :], {"span": other}),
            halo_copy(9 + a, src.at[0, :, a, edge, :], src.at[0, :, a, 32:40, :], {"span": other}),
        )
        for a in range(4)
    ]
    last_halo = halo_copy(13, inv.at[0, edge, :], inv.at[0, 32:40, :], {"span": other})

    slices = []
    for a in range(4):
        slices += [(buf, (0,), (c, a)) for c in range(5)]
    for a in range(4):
        slices += [(cpl, (), (d, a)) for d in range(6) if (d, a) not in ((0, 3), (1, 0))]
        slices += [(src, (), (c, a)) for c in range(5)]
    slices.append((inv, (), ()))
    firsts = (0, 20, 30, 41, 52, 63)

    def pack():
        for tile in range(4):
            to_right = jnp.zeros((32, 128), F32)
            to_left = jnp.zeros((32, 128), F32)
            for k, (ref, before, after) in enumerate(slices[16 * tile : 16 * tile + 16]):
                x = ref[before + (0,) + after + (slice(0, 32), slice(None))]
                mine = (lane >> 3) == k
                to_left = jnp.where(mine, pltpu.roll(x, 8 * k, 1) if k else x, to_left)
                shift = (8 * k + 8) % 128
                to_right = jnp.where(mine, pltpu.roll(x, shift, 1) if shift else x, to_right)
            right_out[tile] = to_right
            left_out[tile] = to_left

    def unpack(group):
        for i in range(firsts[group], firsts[group + 1]):
            ref, before, after = slices[i]
            tile, k = i // 16, i % 16
            x, y = from_right[tile], from_left[tile]
            x = pltpu.roll(x, 128 - 8 * k, 1) if k else x
            y = pltpu.roll(y, 120 - 8 * k, 1) if k < 15 else y
            ref[before + (1,) + after] = jnp.where(long_lane < 64, x, y)

    def sweep_layer(n, a, chunks):
        for tile, lo, hi in chunks:
            total = [src[tile, c, a, lo:hi] for c in range(5)]
            at = long_lane[lo:hi]

            def add(direction, neighbours):
                weight = cpl[tile, direction, a, lo:hi]
                for c in range(5):
                    mixed = jac[0, c, 0, direction] * neighbours[0]
                    for j in range(1, 5):
                        mixed = mixed + jac[j, c, 0, direction] * neighbours[j]
                    total[c] = total[c] + weight * mixed

            if a < 3:
                add(0, [buf[n, tile, j, a + 1, lo:hi] for j in range(5)])
            if a > 0:
                add(1, [buf[n, tile, j, a - 1, lo:hi] for j in range(5)])
            columns = [buf[n, tile, j, a] for j in range(5)]
            add(2, [pltpu.roll(x, 39, 0)[lo:hi] for x in columns])
            add(3, [pltpu.roll(x, 1, 0)[lo:hi] for x in columns])
            cells = [buf[n, tile, j, a, lo:hi] for j in range(5)]
            beside = [buf[n, 1 - tile, j, a, lo:hi] for j in range(5)]
            for direction, shift, end in ((4, 127, 127), (5, 1, 0)):
                add(
                    direction,
                    [
                        jnp.where(at == end, pltpu.roll(y, shift, 1), pltpu.roll(x, shift, 1))
                        for x, y in zip(cells, beside)
                    ],
                )
            for c in range(5):
                if n == ITERS - 1:
                    result[c, a] = total[c]
                else:
                    buf[n + 1, tile, c, a, lo:hi] = total[c]

    main = ((0, 0, 32),)
    rest = ((0, 32, 40), (1, 0, 40))
    full = ((0, 0, 40), (1, 0, 40))

    def coefs_of(n, lo, hi):
        coefs = coef_in[n, 0, lo:hi]
        for o in range(1, pitches):
            coefs = coefs + coef_in[n, o, lo:hi]
        return split(coefs)

    def add_boundary(n, chunks):
        for tile, lo, hi in chunks:
            high, low = coefs_of(n, lo, hi)
            table = (slice(None), slice(640 * tile, 640 * tile + 640))
            field = dot(high, syn_hi[table]) + (dot(low, syn_hi[table]) + dot(high, syn_lo[table]))
            for c in range(5):
                share = field[:, 128 * c : 128 * c + 128] * inv[tile, lo:hi]
                if n == ITERS - 1:
                    result[c, 3] = result[c, 3] + share
                else:
                    buf[n + 1, tile, c, 3, lo:hi] = buf[n + 1, tile, c, 3, lo:hi] + share

    loads[0].wait()
    project(0)

    for copy in loads[1:4]:
        copy.wait()
    keep_next = jnp.where((srow == 31) & (span == 1), 0.0, 1.0)
    keep_prev = jnp.where((srow == 0) & (span == 0), 0.0, 1.0)
    for a in range(4):
        diag = dmp_raw[a]
        for d in range(6):
            diag = diag + cpl_raw[d, a]
        inverse = 1.0 / diag
        for d in range(6):
            weight = cpl_raw[d, a] * inverse
            if d == 2:
                weight = weight * keep_next
            if d == 3:
                weight = weight * keep_prev
            cpl[0, d, a, 0:32] = weight
        for c in range(5):
            src[0, c, a, 0:32] = src_raw[c, a] * inverse
        if a == 3:
            inv[0, 0:32] = inverse
    pack()

    pl.semaphore_wait(
        barrier, 5 + 2 * pitches * ((row > 0).astype(I32) + (row < last).astype(I32))
    )
    for copy in side_halos:
        copy.start()
    start_halo.start()
    for pair in layer_halos:
        for copy in pair:
            copy.start()
    last_halo.start()
    send_coefs(0)

    for copy in loads[4:]:
        copy.wait()
    for j in range(5):
        for c in range(5):
            gmix[5 * j + c : 5 * j + c + 1, 0:64] = gre[j, c, pl.ds(face, 1), :]
            gmix[5 * j + c : 5 * j + c + 1, 64:128] = gim[j, c, pl.ds(face, 1), :]
    gmix[25:32, :] = jnp.zeros((7, 128), F32)
    one = (orders[0:1, :] + 2) * 5 + (orders[1:2, :] + 2)
    mode_of = jnp.concatenate([one, one], axis=1)
    comp, u, mode, number = lane_modes(wide_row, blades[face], blades[face + 1])
    same = jnp.where(mode_of == mode, 1.0, 0.0)
    opposite = jnp.where(mode_of == 24 - mode, 1.0, 0.0)
    either = jnp.maximum(same, opposite)
    signed = same - opposite
    in_real = wide_lane < 64
    cosine_row = u >= 12
    for_cos = jnp.where(
        cosine_row, jnp.where(in_real, either, 0.0), jnp.where(in_real, 0.0, -signed)
    )
    for_sin = jnp.where(
        cosine_row, jnp.where(in_real, 0.0, -signed), jnp.where(in_real, -either, 0.0)
    )
    contract = (((1,), (1,)), ((), ()))
    cos_mix = lax.dot_general(
        for_cos, gmix[...], contract, precision=lax.Precision.HIGHEST, preferred_element_type=F32
    )
    sin_mix = lax.dot_general(
        for_sin, gmix[...], contract, precision=lax.Precision.HIGHEST, preferred_element_type=F32
    )
    pick = lax.broadcasted_iota(I32, (128, 32), 1)
    pick_comp = (lax.broadcasted_iota(I32, (128, 32), 0) * 41) >> 10
    beside = jnp.where(lane[0:1] < 64, donors[1], donors[2])
    for tile, cells in enumerate((donors[0], beside)):
        turns = number * cells
        cosine = jnp.where(comp < 5, sine(turns + length // 4, length), 0.0)
        minus = jnp.where(comp < 5, sine(turns, length), 0.0)
        for c in range(5):
            chosen = pick == 5 * pick_comp + c
            on_cos = jnp.sum(jnp.where(chosen, cos_mix, 0.0), axis=1, keepdims=True)
            on_sin = jnp.sum(jnp.where(chosen, sin_mix, 0.0), axis=1, keepdims=True)
            high, low = split(on_cos * cosine + on_sin * minus)
            first = 640 * tile + 128 * c
            syn_hi[:, first : first + 128] = high
            syn_lo[:, first : first + 128] = low

    def wait_sides():
        for copy in side_halos:
            copy.wait_recv()

    def wait_layer(a):
        for copy in layer_halos[a]:
            copy.wait_recv()

    def wait_start():
        start_halo.wait_recv()

    wait_sides()
    unpack(0)
    unpack(1)
    wait_start()
    wait_layer(0)
    sweep_layer(0, 0, full)
    project(1)
    send_coefs(1)
    unpack(2)
    wait_layer(1)
    sweep_layer(0, 1, full)
    sweep_layer(1, 0, full)
    project(2)
    send_coefs(2)
    unpack(3)
    wait_layer(2)
    sweep_layer(0, 2, full)
    sweep_layer(1, 1, full)
    sweep_layer(2, 0, full)
    project(3)
    send_coefs(3)

    sweep_layer(0, 3, main)
    wait_coefs(0)
    add_boundary(0, main)
    sweep_layer(1, 2, main)
    sweep_layer(2, 1, main)
    sweep_layer(3, 0, main)
    project(4)
    send_coefs(4)

    unpack(4)
    wait_layer(3)
    last_halo.wait_recv()
    sweep_layer(0, 3, rest)
    add_boundary(0, rest)
    sweep_layer(1, 2, rest)
    sweep_layer(2, 1, rest)
    sweep_layer(3, 0, rest)
    sweep_layer(1, 3, full)
    wait_coefs(1)
    add_boundary(1, full)
    sweep_layer(2, 2, full)
    sweep_layer(2, 3, full)
    wait_coefs(2)
    add_boundary(2, full)
    sweep_layer(3, 1, full)
    sweep_layer(3, 2, full)
    sweep_layer(3, 3, full)
    stores = []

    def store(a):
        copy = pltpu.make_async_copy(result.at[:, a], out_hbm.at[:, a], store_sem.at[a])
        copy.start()
        stores.append(copy)

    for a in (0, 1):
        sweep_layer(4, a, main)
        store(a)
    wait_coefs(3)
    add_boundary(3, full)
    sweep_layer(4, 2, main)
    store(2)
    sweep_layer(4, 3, main)
    wait_coefs(4)
    add_boundary(4, main)
    store(3)

    for copy in side_halos + [start_halo, last_halo]:
        copy.wait_send()
    for pair in layer_halos:
        for copy in pair:
            copy.wait_send()

    @pl.when(row > 0)
    def _():
        for n in range(ITERS):
            for part in parts_of(n):
                for o in range(pitches):
                    coef_copy(n, part, o).wait_send()

    for copy in stores:
        copy.wait()


def on_device(
    rows,
    pitches,
    adjoint_start,
    source,
    couplings,
    damping,
    jacobians,
    giles_real,
    giles_imag,
    blades,
    mode_orders,
    cell_map,
):
    faces = rows - 1
    anywhere = pl.BlockSpec(memory_space=pl.ANY)
    scalars = pl.BlockSpec(memory_space=pltpu.SMEM)
    dma = pltpu.SemaphoreType.DMA
    scratch = [
        pltpu.VMEM((ITERS, 2, 5, 4, 40, 128), F32),
        pltpu.VMEM((2, 5, 4, 40, 128), F32),
        pltpu.VMEM((2, 6, 4, 40, 128), F32),
        pltpu.VMEM((2, 40, 128), F32),
        pltpu.VMEM((5, 4, 32, 128), F32),
        pltpu.VMEM((6, 4, 32, 128), F32),
        pltpu.VMEM((4, 32, 128), F32),
        pltpu.VMEM((5, 4, 32, 128), F32),
        pltpu.VMEM((5, 5, faces, 64), F32),
        pltpu.VMEM((5, 5, faces, 64), F32),
        pltpu.VMEM((2, 64), I32),
        pltpu.VMEM((3, 1, 128), I32),
        pltpu.VMEM((32, 128), F32),
        pltpu.VMEM((128, 128), BF16),
        pltpu.VMEM((128, 128), BF16),
        pltpu.VMEM((128, 1280), BF16),
        pltpu.VMEM((128, 1280), BF16),
        pltpu.VMEM((ITERS, 32, 128), F32),
        pltpu.VMEM((ITERS, pitches, 40, 128), F32),
        pltpu.VMEM((4, 32, 128), F32),
        pltpu.VMEM((4, 32, 128), F32),
        pltpu.VMEM((4, 40, 128), F32),
        pltpu.VMEM((4, 40, 128), F32),
        dma((10,)),
        dma((4,)),
        dma((ITERS, 2, pitches)),
        dma((ITERS, 2, pitches)),
        dma((14,)),
        dma((14,)),
    ]

    def body(*refs):
        kernel(rows, pitches, *refs)

    return pl.pallas_call(
        body,
        name="sweeps",
        out_shape=jax.ShapeDtypeStruct(adjoint_start.shape, F32),
        in_specs=[
            anywhere,
            anywhere,
            anywhere,
            anywhere,
            scalars,
            anywhere,
            anywhere,
            scalars,
            anywhere,
            anywhere,
        ],
        out_specs=anywhere,
        scratch_shapes=scratch,
        compiler_params=pltpu.CompilerParams(collective_id=0, has_side_effects=True),
    )(
        adjoint_start,
        source,
        couplings,
        damping,
        jnp.transpose(jacobians, (2, 3, 0, 1)),
        jnp.transpose(giles_real, (2, 3, 0, 1)),
        jnp.transpose(giles_imag, (2, 3, 0, 1)),
        blades,
        jnp.transpose(mode_orders, (0, 2, 1)),
        cell_map,
    )


def solution(mesh):
    rows, pitches = mesh.shape["row"], mesh.shape["pitch"]

    def step(*args):
        return on_device(rows, pitches, *args)

    placed = (
        P(None, "row", "span", "pitch"),
        P(None, "row", "span", "pitch"),
        P(None, "row", "span", "pitch"),
        P("row", "span", "pitch"),
        P("row", None, None, None),
        P(),
        P(),
        P(),
        P(),
        P("row", None),
    )
    return jax.shard_map(
        step,
        mesh=mesh,
        in_specs=placed,
        out_specs=P(None, "row", "span", "pitch"),
        check_vma=False,
    )
```

time: 49.8 us -> 38.4 us (0.77)
  the two profiles are of different devices: /device:TPU:2 before, /device:TPU:1 now
where the time goes in v2:
time: 38.4 us; the launch traced here: 38.2 us
  Pallas kernels  36.4 us (95%)
  local copies, waits for them, and re-layouts  1.72 us (4%)
    pallas_call x1, Pallas kernels, on_device(): pl.pallas_call(body, name='sweeps', out_shape=jax.ShapeDtypeStruct(adjoin...  36.4 us
    unnamed x1, local copies, waits for them, and re-layouts  1.72 us

profile of v2, /device:TPU:1, one launch (start us, length us, event | category | flops | bytes accessed | tf_op | source)
XLA Modules:
  0.0 38.2 jit_solution(7833082164043690878)
XLA Ops:
  0.0 36.4 %sweeps.1 = f32[5,4,32,128]{3,2,1,0:T(8,128)} custom-call(f32[5,4,32,128]{3,2,1,0:T(8,128)} %refs_0_.1, f32[5,4,32,128]{3,2,1,0:T(8,128)} %refs_1_.1, f32[6,4,32,128]{3,2,1,0:T(8,128)} %refs_2_.1, f32[4,32,128]{2,1,0:T(8,128)} %refs_3_.1, f32[5,5,1,6]{3,2,1,0:T(1,128)} %bitcast.7, f32[5,5,15,64]{3,2,1,0:T(8,128)} %bitcast.4, f32[5,5,15,64]{3,2,1,0:T(8,128)} %bitcast.5, ...), custom_call_target="tpu_custom_call" | custom-call | tf_op jit(solution)/shard_map/sweeps/pallas_call | solution.py:552
  36.5 1.7 %copy.12 = f32[5,4,32,128]{3,2,1,0:T(8,128)} copy(f32[5,4,32,128]{3,2,1,0:T(8,128)} %sweeps.1) | data formatting | bytes 655360

commit v3 on v2

v3 whole, which is shorter than its diff:
```python
import math

import jax
import jax.numpy as jnp
from jax import lax
from jax.experimental import pallas as pl
from jax.experimental.pallas import tpu as pltpu
from jax.sharding import PartitionSpec as P

ITERS = 5
MESH = pl.DeviceIdType.MESH
F32 = jnp.float32
BF16 = jnp.bfloat16
I32 = jnp.int32

def sine(turns, length):
    half, quarter = length // 2, length // 4
    t = ((turns + half) & (length - 1)) - half
    t = jnp.where(t > quarter, half - t, jnp.where(t < -quarter, -half - t, t))
    x = t.astype(F32) * (2.0 * math.pi / length)
    y = x * x
    poly = 1.0 / 6227020800.0
    for c in (-1.0 / 39916800.0, 1.0 / 362880.0, -1.0 / 5040.0, 1.0 / 120.0, -1.0 / 6.0):
        poly = poly * y + c
    return x + x * (y * poly)


def split(x):
    high = x.astype(BF16)
    return high, (x - high.astype(F32)).astype(BF16)


def dot(a, b):
    return jnp.dot(a, b, preferred_element_type=F32)


def lane_modes(index, blades_low, blades_high):
    comp = (index * 41) >> 10
    u = index - 25 * comp
    mode = jnp.where(u >= 12, u, 24 - u)
    first = (mode * 13) >> 6
    second = mode - 5 * first
    return comp, u, mode, (first - 2) * blades_low + (second - 2) * blades_high


def kernel(
    rows,
    pitches,
    adj_hbm,
    src_hbm,
    cpl_hbm,
    dmp_hbm,
    jac_hbm,
    gr_hbm,
    gi_hbm,
    blades_hbm,
    ord_hbm,
    map_hbm,
    result,
    jac,
    blades,
    buf,
    cpl,
    inv,
    src_raw,
    cpl_raw,
    dmp_raw,
    giles,
    orders,
    donors,
    gmix,
    fwd_hi,
    fwd_lo,
    syn_hi,
    syn_lo,
    coef_out,
    gathered,
    reduced,
    coef_in,
    last_in,
    right_out,
    left_out,
    from_left,
    from_right,
    gauge,
    load_sem,
    sent,
    gather_recv,
    spread_recv,
    last_recv,
    halo_recv,
):
    row, span, pitch = lax.axis_index("row"), lax.axis_index("span"), lax.axis_index("pitch")
    length = 128 * pitches
    last = rows - 1
    right, left = lax.rem(pitch + 1, pitches), lax.rem(pitch + pitches - 1, pitches)
    face = jnp.minimum(row, rows - 2)
    upstream = jnp.maximum(row - 1, 0)
    other = 1 - span
    edge = pl.ds(pl.multiple_of(24 * other, 8), 8)
    near = pl.ds(pl.multiple_of(28 * other, 4), 4)
    far = pl.ds(pl.multiple_of(32 + 4 * other, 4), 4)

    barrier = pltpu.get_barrier_semaphore()

    def greet(target):
        pl.semaphore_signal(barrier, inc=1, device_id=target, device_id_type=MESH)

    offsets = sorted(range(pitches), key=lambda o: -min(o, pitches - o))

    def partners_of(there):
        for o in offsets:
            for half in (span, other):
                greet({"row": there, "span": half, "pitch": lax.rem(pitch + o, pitches)})

    def donor_load(slot, where):
        cells = pl.ds(pl.multiple_of(where * 128, 128), 128)
        return pltpu.make_async_copy(map_hbm.at[:, cells], donors.at[slot], load_sem.at[6])

    loads = [
        pltpu.make_async_copy(adj_hbm, buf.at[0, 0, :, :, 0:32, :], load_sem.at[0]),
        pltpu.make_async_copy(cpl_hbm, cpl_raw, load_sem.at[1]),
        pltpu.make_async_copy(dmp_hbm, dmp_raw, load_sem.at[2]),
        pltpu.make_async_copy(src_hbm, src_raw, load_sem.at[3]),
        pltpu.make_async_copy(blades_hbm, blades, load_sem.at[7]),
        pltpu.make_async_copy(jac_hbm, jac, load_sem.at[8]),
        pltpu.make_async_copy(ord_hbm.at[face], orders, load_sem.at[4]),
    ]
    for copy in loads:
        copy.start()
    for copy in (
        pltpu.make_async_copy(gr_hbm, giles.at[0], load_sem.at[5]),
        pltpu.make_async_copy(gi_hbm, giles.at[1], load_sem.at[5]),
        donor_load(0, pitch),
        donor_load(1, right),
        donor_load(2, left),
    ):
        copy.start()

    @pl.when(row > 0)
    def _():
        partners_of(row - 1)

    @pl.when(row < last)
    def _():
        partners_of(row + 1)

    greet({"span": other})
    for o in range(1, pitches):
        greet({"pitch": lax.rem(pitch + o, pitches)})
    for side in (right, left):
        greet({"span": other, "pitch": side})

    def take(semaphore, tiles):
        there = gauge.at[0:tiles]
        pltpu.make_async_copy(there, there, semaphore).wait()

    lane = lax.broadcasted_iota(I32, (32, 128), 1)
    long_lane = lax.broadcasted_iota(I32, (40, 128), 1)
    srow = lax.broadcasted_iota(I32, (32, 128), 0)
    block = (lane * 41) >> 10

    loads[4].wait()

    wide_lane = lax.broadcasted_iota(I32, (128, 128), 1)
    wide_row = lax.broadcasted_iota(I32, (128, 128), 0)
    comp, u, mode, number = lane_modes(wide_lane, blades[upstream], blades[upstream + 1])
    turns = number * (wide_row + pitch * 128) + jnp.where(u >= 12, length // 4, length // 2)
    table = jnp.where(comp < 5, sine(turns, length) * (2.0 / length), 0.0)
    high, low = split(table)
    fwd_hi[...] = high
    fwd_lo[...] = low

    @pl.when(row == last)
    def _():
        coef_in[...] = jnp.zeros_like(coef_in)
        last_in[...] = jnp.zeros_like(last_in)

    spread = pitches // 4
    stations = lax.div(pitch, spread)
    at_edge = stations == 3 * other

    def gather_copy(n, part):
        return pltpu.make_async_remote_copy(
            src_ref=coef_out.at[n, 8 * part : 8 * part + 8],
            dst_ref=gathered.at[n, pitch],
            send_sem=sent.at[1],
            recv_sem=gather_recv.at[n],
            device_id={"pitch": part * spread + n % spread},
            device_id_type=MESH,
        )

    def adds(n):
        return (row > 0) & (lax.rem(pitch, spread) == n % spread)

    def send_coefs(n):
        for part in range(4):
            target = part * spread + n % spread

            @pl.when((row > 0) & (pitch != target))
            def _():
                gather_copy(n, part).start()

            @pl.when((row > 0) & (pitch == target))
            def _():
                gathered[n, pitch] = coef_out[n, 8 * part : 8 * part + 8]

    def spread_copy(n, beyond, target):
        slot = 4 if beyond else stations
        landing = pl.ds(pl.multiple_of(8 * slot, 8), 8)
        return pltpu.make_async_remote_copy(
            src_ref=reduced.at[n],
            dst_ref=coef_in.at[n, landing],
            send_sem=sent.at[1 + beyond],
            recv_sem=spread_recv.at[n],
            device_id={"row": upstream, "span": other if beyond else span, "pitch": target},
            device_id_type=MESH,
        )

    def reduce_coefs(n):
        @pl.when(adds(n))
        def _():
            take(gather_recv.at[n], pitches - 1)
            total = gathered[n, 0]
            for o in range(1, pitches):
                total = total + gathered[n, o]
            reduced[n] = total
            for o in offsets:
                spread_copy(n, 0, lax.rem(pitch + o, pitches)).start()

            @pl.when(at_edge)
            def _():
                for o in offsets:
                    spread_copy(n, 1, lax.rem(pitch + o, pitches)).start()

    def wait_coefs(n):
        @pl.when(row < last)
        def _():
            take(spread_recv.at[n], 5)

    def last_copy(target):
        return pltpu.make_async_remote_copy(
            src_ref=coef_out.at[ITERS - 1],
            dst_ref=last_in.at[pitch],
            send_sem=sent.at[1],
            recv_sem=last_recv.at[0],
            device_id={"row": upstream, "pitch": target},
            device_id_type=MESH,
        )

    def send_last():
        @pl.when(row > 0)
        def _():
            for o in offsets:
                last_copy(lax.rem(pitch + o, pitches)).start()

    def wait_last():
        @pl.when(row < last)
        def _():
            take(last_recv.at[0], 4 * pitches)

    def project(n):
        strip = buf[n, 0, :, 0, 0:32, :].reshape(160, 128)
        high, low = split(strip)
        both = dot(high, fwd_hi[...]) + (dot(low, fwd_hi[...]) + dot(high, fwd_lo[...]))
        total = jnp.zeros((32, 128), F32)
        for c in range(5):
            total = total + jnp.where(block == c, both[32 * c : 32 * c + 32], 0.0)
        coef_out[n] = total

    def halo_copy(i, source, landing, target):
        return pltpu.make_async_remote_copy(
            src_ref=source,
            dst_ref=landing,
            send_sem=sent.at[0],
            recv_sem=halo_recv.at[i],
            device_id=target,
            device_id_type=MESH,
        )

    def side_copies(half):
        tiles = slice(2 * half, 2 * half + 2)
        below, beyond = slice(0, 32), slice(32, 40)
        return [
            halo_copy(
                half, right_out.at[tiles], from_left.at[tiles, below], {"pitch": right}
            ),
            halo_copy(
                half, left_out.at[tiles], from_right.at[tiles, below], {"pitch": left}
            ),
            halo_copy(
                half,
                right_out.at[tiles, edge],
                from_left.at[tiles, beyond],
                {"span": other, "pitch": right},
            ),
            halo_copy(
                half,
                left_out.at[tiles, edge],
                from_right.at[tiles, beyond],
                {"span": other, "pitch": left},
            ),
        ]

    side_halos = [side_copies(half) for half in (0, 1)]
    start_halo = halo_copy(
        2, buf.at[0, 0, :, :, edge, :], buf.at[0, 0, :, :, 32:40, :], {"span": other}
    )
    layer_halos = [
        halo_copy(3 + a, cpl.at[0, :, a, near, :], cpl.at[0, :, a, far, :], {"span": other})
        for a in range(4)
    ]
    last_halo = halo_copy(7, inv.at[0, edge, :], inv.at[0, 32:40, :], {"span": other})

    slices = []
    for a in range(4):
        slices += [(buf, (0,), (c, a)) for c in range(5)]
    for a in range(4):
        slices += [(cpl, (), (d, a)) for d in range(6) if (d, a) not in ((0, 3), (1, 0))]
        slices += [(cpl, (), (6 + c, a)) for c in range(5)]
    slices.append((inv, (), ()))
    firsts = (0, 20, 30, 41, 52, 63)

    def pack():
        low_end = (lane & 15) < 8
        for tile in range(4):
            halves = []
            for first in (16 * tile, 16 * tile + 8):
                packed = jnp.zeros((32, 128), F32)
                for k, (ref, before, after) in enumerate(slices[first : first + 8]):
                    x = ref[before + (0,) + after + (slice(0, 32), slice(None))]
                    shift = (16 * k + 8) % 128
                    packed = jnp.where((lane >> 4) == k, pltpu.roll(x, shift, 1), packed)
                halves.append(packed)
            right_out[tile] = jnp.where(low_end, halves[0], pltpu.roll(halves[1], 8, 1))
            left_out[tile] = jnp.where(low_end, pltpu.roll(halves[1], 120, 1), halves[0])

    def unpack(group):
        low_end = (long_lane & 15) < 8
        joined = {}
        for i in range(firsts[group], firsts[group + 1]):
            ref, before, after = slices[i]
            tile, half, k = i // 16, (i // 8) % 2, i % 8
            if (tile, half) not in joined:
                x, y = from_left[tile], from_right[tile]
                if half:
                    x, y = pltpu.roll(x, 120, 1), pltpu.roll(y, 8, 1)
                joined[tile, half] = jnp.where(low_end, x, y)
            ref[before + (1,) + after] = pltpu.roll(joined[tile, half], 120 - 16 * k, 1)

    def sweep_layer(n, a, chunks):
        for tile, lo, hi in chunks:
            total = [cpl[tile, 6 + c, a, lo:hi] for c in range(5)]
            at = long_lane[lo:hi]

            def add(direction, neighbours):
                weight = cpl[tile, direction, a, lo:hi]
                for c in range(5):
                    mixed = jac[0, c, 0, direction] * neighbours[0]
                    for j in range(1, 5):
                        mixed = mixed + jac[j, c, 0, direction] * neighbours[j]
                    total[c] = total[c] + weight * mixed

            if a < 3:
                add(0, [buf[n, tile, j, a + 1, lo:hi] for j in range(5)])
            if a > 0:
                add(1, [buf[n, tile, j, a - 1, lo:hi] for j in range(5)])
            columns = [buf[n, tile, j, a] for j in range(5)]
            add(2, [pltpu.roll(x, 39, 0)[lo:hi] for x in columns])
            add(3, [pltpu.roll(x, 1, 0)[lo:hi] for x in columns])
            cells = [buf[n, tile, j, a, lo:hi] for j in range(5)]
            beside = [buf[n, 1 - tile, j, a, lo:hi] for j in range(5)]
            for direction, shift, end in ((4, 127, 127), (5, 1, 0)):
                add(
                    direction,
                    [
                        jnp.where(at == end, pltpu.roll(y, shift, 1), pltpu.roll(x, shift, 1))
                        for x, y in zip(cells, beside)
                    ],
                )
            for c in range(5):
                if n == ITERS - 1:
                    result[c, a] = total[c]
                else:
                    buf[n + 1, tile, c, a, lo:hi] = total[c]

    main = ((0, 0, 32),)
    full = ((0, 0, 40), (1, 0, 40))

    def coefs_of(n, lo, hi):
        if n < ITERS - 1:
            return split(coef_in[n, lo:hi])
        coefs = last_in[0, lo:hi]
        for o in range(1, pitches):
            coefs = coefs + last_in[o, lo:hi]
        return split(coefs)

    def add_boundary(n, chunks):
        for tile, lo, hi in chunks:
            high, low = coefs_of(n, lo, hi)
            table = (slice(None), slice(640 * tile, 640 * tile + 640))
            field = dot(high, syn_hi[table]) + (dot(low, syn_hi[table]) + dot(high, syn_lo[table]))
            for c in range(5):
                share = field[:, 128 * c : 128 * c + 128] * inv[tile, lo:hi]
                if n == ITERS - 1:
                    result[c, 3] = result[c, 3] + share
                else:
                    buf[n + 1, tile, c, 3, lo:hi] = buf[n + 1, tile, c, 3, lo:hi] + share

    for copy in loads[0:4]:
        copy.wait()
    keep_next = jnp.where((srow == 31) & (span == 1), 0.0, 1.0)
    keep_prev = jnp.where((srow == 0) & (span == 0), 0.0, 1.0)
    for a in range(4):
        diag = dmp_raw[a]
        for d in range(6):
            diag = diag + cpl_raw[d, a]
        inverse = 1.0 / diag
        for d in range(6):
            weight = cpl_raw[d, a] * inverse
            if d == 2:
                weight = weight * keep_next
            if d == 3:
                weight = weight * keep_prev
            cpl[0, d, a, 0:32] = weight
        for c in range(5):
            cpl[0, 6 + c, a, 0:32] = src_raw[c, a] * inverse
        if a == 3:
            inv[0, 0:32] = inverse
    pack()

    linked = (row > 0).astype(I32) + (row < last).astype(I32)
    pl.semaphore_wait(barrier, 2 + pitches + 2 * pitches * linked)
    for copy in side_halos[0]:
        copy.start()
    start_halo.start()
    layer_halos[0].start()
    for copy in side_halos[1]:
        copy.start()
    for copy in layer_halos[1:]:
        copy.start()
    last_halo.start()
    project(0)
    send_coefs(0)

    loads[5].wait()
    loads[6].wait()
    pltpu.make_async_copy(giles, giles, load_sem.at[5]).wait()
    pltpu.make_async_copy(donors, donors, load_sem.at[6]).wait()
    for j in range(5):
        for c in range(5):
            gmix[5 * j + c : 5 * j + c + 1, 0:64] = giles[0, j, c, pl.ds(face, 1), :]
            gmix[5 * j + c : 5 * j + c + 1, 64:128] = giles[1, j, c, pl.ds(face, 1), :]
    gmix[25:32, :] = jnp.zeros((7, 128), F32)
    one = (orders[0:1, :] + 2) * 5 + (orders[1:2, :] + 2)
    mode_of = jnp.concatenate([one, one], axis=1)
    comp, u, mode, number = lane_modes(wide_row, blades[face], blades[face + 1])
    same = jnp.where(mode_of == mode, 1.0, 0.0)
    opposite = jnp.where(mode_of == 24 - mode, 1.0, 0.0)
    either = jnp.maximum(same, opposite)
    signed = same - opposite
    in_real = wide_lane < 64
    cosine_row = u >= 12
    for_cos = jnp.where(
        cosine_row, jnp.where(in_real, either, 0.0), jnp.where(in_real, 0.0, -signed)
    )
    for_sin = jnp.where(
        cosine_row, jnp.where(in_real, 0.0, -signed), jnp.where(in_real, -either, 0.0)
    )
    contract = (((1,), (1,)), ((), ()))
    cos_mix = lax.dot_general(
        for_cos, gmix[...], contract, precision=lax.Precision.HIGHEST, preferred_element_type=F32
    )
    sin_mix = lax.dot_general(
        for_sin, gmix[...], contract, precision=lax.Precision.HIGHEST, preferred_element_type=F32
    )
    pick = lax.broadcasted_iota(I32, (128, 32), 1)
    pick_comp = (lax.broadcasted_iota(I32, (128, 32), 0) * 41) >> 10
    beside = jnp.where(lane[0:1] < 64, donors[1], donors[2])
    for tile, cells in enumerate((donors[0], beside)):
        turns = number * cells
        cosine = jnp.where(comp < 5, sine(turns + length // 4, length), 0.0)
        minus = jnp.where(comp < 5, sine(turns, length), 0.0)
        for c in range(5):
            chosen = pick == 5 * pick_comp + c
            on_cos = jnp.sum(jnp.where(chosen, cos_mix, 0.0), axis=1, keepdims=True)
            on_sin = jnp.sum(jnp.where(chosen, sin_mix, 0.0), axis=1, keepdims=True)
            high, low = split(on_cos * cosine + on_sin * minus)
            first = 640 * tile + 128 * c
            syn_hi[:, first : first + 128] = high
            syn_lo[:, first : first + 128] = low

    def wait_sides(half):
        take(halo_recv.at[half], 20)

    def wait_layer(a):
        layer_halos[a].wait_recv()

    def wait_scale():
        last_halo.wait_recv()

    def wait_start():
        start_halo.wait_recv()

    reduce_coefs(0)
    wait_sides(0)
    unpack(0)
    unpack(1)
    wait_start()
    wait_layer(0)
    sweep_layer(0, 0, full)
    project(1)
    send_coefs(1)
    wait_sides(1)
    unpack(2)
    wait_layer(1)
    sweep_layer(0, 1, full)
    sweep_layer(1, 0, full)
    project(2)
    send_coefs(2)
    unpack(3)
    wait_layer(2)
    sweep_layer(0, 2, full)
    sweep_layer(1, 1, full)
    sweep_layer(2, 0, full)
    project(3)
    send_coefs(3)
    reduce_coefs(1)

    unpack(4)
    wait_layer(3)
    wait_scale()
    sweep_layer(0, 3, full)
    wait_coefs(0)
    add_boundary(0, full)
    reduce_coefs(2)
    sweep_layer(1, 2, full)
    sweep_layer(2, 1, full)
    sweep_layer(3, 0, full)
    project(4)
    send_last()

    sweep_layer(1, 3, full)
    reduce_coefs(3)
    wait_coefs(1)
    add_boundary(1, full)
    sweep_layer(2, 2, full)
    sweep_layer(2, 3, full)
    sweep_layer(3, 1, full)
    sweep_layer(4, 0, main)
    wait_coefs(2)
    add_boundary(2, full)
    sweep_layer(3, 2, full)
    sweep_layer(4, 1, main)
    sweep_layer(3, 3, full)
    wait_coefs(3)
    add_boundary(3, full)
    sweep_layer(4, 2, main)
    sweep_layer(4, 3, main)
    wait_last()
    add_boundary(4, main)

    own = (ITERS - 1) // spread
    take(sent.at[0], 83)

    @pl.when(row > 0)
    def _():
        take(sent.at[1], 16 - own + own * pitches + 4 * pitches)

    @pl.when((row > 0) & at_edge)
    def _():
        take(sent.at[2], own * pitches)


def on_device(
    rows,
    pitches,
    adjoint_start,
    source,
    couplings,
    damping,
    jacobians,
    giles_real,
    giles_imag,
    blades,
    mode_orders,
    cell_map,
):
    faces = rows - 1
    anywhere = pl.BlockSpec(memory_space=pl.ANY)
    dma = pltpu.SemaphoreType.DMA
    scratch = [
        pltpu.SMEM((5, 5, 1, 6), F32),
        pltpu.SMEM((rows,), I32),
        pltpu.VMEM((ITERS, 2, 5, 4, 40, 128), F32),
        pltpu.VMEM((2, 11, 4, 40, 128), F32),
        pltpu.VMEM((2, 40, 128), F32),
        pltpu.VMEM((5, 4, 32, 128), F32),
        pltpu.VMEM((6, 4, 32, 128), F32),
        pltpu.VMEM((4, 32, 128), F32),
        pltpu.VMEM((2, 5, 5, faces, 64), F32),
        pltpu.VMEM((2, 64), I32),
        pltpu.VMEM((3, 1, 128), I32),
        pltpu.VMEM((32, 128), F32),
        pltpu.VMEM((128, 128), BF16),
        pltpu.VMEM((128, 128), BF16),
        pltpu.VMEM((128, 1280), BF16),
        pltpu.VMEM((128, 1280), BF16),
        pltpu.VMEM((ITERS, 32, 128), F32),
        pltpu.VMEM((ITERS - 1, pitches, 8, 128), F32),
        pltpu.VMEM((ITERS - 1, 8, 128), F32),
        pltpu.VMEM((ITERS - 1, 40, 128), F32),
        pltpu.VMEM((pitches, 32, 128), F32),
        pltpu.VMEM((4, 32, 128), F32),
        pltpu.VMEM((4, 32, 128), F32),
        pltpu.VMEM((4, 40, 128), F32),
        pltpu.VMEM((4, 40, 128), F32),
        pltpu.VMEM((83, 8, 128), F32),
        dma((9,)),
        dma((3,)),
        dma((ITERS - 1,)),
        dma((ITERS - 1,)),
        dma((1,)),
        dma((8,)),
    ]

    def body(*refs):
        kernel(rows, pitches, *refs)

    return pl.pallas_call(
        body,
        name="sweeps",
        out_shape=pltpu.VMEM(adjoint_start.shape, F32),
        in_specs=[anywhere] * 10,
        out_specs=pl.BlockSpec(memory_space=pltpu.VMEM),
        scratch_shapes=scratch,
        compiler_params=pltpu.CompilerParams(collective_id=0, has_side_effects=True),
    )(
        adjoint_start,
        source,
        couplings,
        damping,
        jnp.transpose(jacobians, (2, 3, 0, 1)),
        jnp.transpose(giles_real, (2, 3, 0, 1)),
        jnp.transpose(giles_imag, (2, 3, 0, 1)),
        blades,
        jnp.transpose(mode_orders, (0, 2, 1)),
        cell_map,
    )


def solution(mesh):
    rows, pitches = mesh.shape["row"], mesh.shape["pitch"]

    def step(*args):
        return on_device(rows, pitches, *args)

    placed = (
        P(None, "row", "span", "pitch"),
        P(None, "row", "span", "pitch"),
        P(None, "row", "span", "pitch"),
        P("row", "span", "pitch"),
        P("row", None, None, None),
        P(),
        P(),
        P(),
        P(),
        P("row", None),
    )
    return jax.shard_map(
        step,
        mesh=mesh,
        in_specs=placed,
        out_specs=P(None, "row", "span", "pitch"),
        check_vma=False,
    )
```

time: 38.4 us -> 32.7 us (0.85)
  Pallas kernels: 36.4 us -> 31.8 us
  local copies, waits for them, and re-layouts: 1.72 us -> 0.73 us
    pallas_call x1, Pallas kernels: 36.4 us -> 31.8 us  [on_device(): pl.pallas_call(body, name='sweeps', out_shape=pltpu.VMEM(adjoint_start.sh...]
    unnamed x1, local copies, waits for them, and re-layouts: 1.72 us -> 0.73 us
where the time goes in v3:
time: 32.7 us; the launch traced here: 32.6 us
  Pallas kernels  31.8 us (97%)
  local copies, waits for them, and re-layouts  0.73 us (2%)
    pallas_call x1, Pallas kernels, on_device(): pl.pallas_call(body, name='sweeps', out_shape=pltpu.VMEM(adjoint_start.sh...  31.8 us
    unnamed x1, local copies, waits for them, and re-layouts  0.73 us

profile of v3, /device:TPU:1, one launch (start us, length us, event | category | flops | bytes accessed | tf_op | source)
XLA Modules:
  0.0 32.6 jit_solution(13033728519593947625)
XLA Ops:
  0.0 31.8 %sweeps.1 = f32[5,4,32,128]{3,2,1,0:T(8,128)S(1)} custom-call(f32[5,4,32,128]{3,2,1,0:T(8,128)} %refs_0_.1, f32[5,4,32,128]{3,2,1,0:T(8,128)} %refs_1_.1, f32[6,4,32,128]{3,2,1,0:T(8,128)} %refs_2_.1, f32[4,32,128]{2,1,0:T(8,128)} %refs_3_.1, f32[5,5,1,6]{3,2,1,0:T(1,128)} %bitcast.7, f32[5,5,15,64]{3,2,1,0:T(8,128)} %bitcast.4, f32[5,5,15,64]{3,2,1,0:T(8,128)} %bitcast.5, ...), custom_call_target="tpu_custom_call" | custom-call | tf_op jit(solution)/shard_map/sweeps/pallas_call | solution.py:630
  31.8 0.7 %copy.12 = f32[5,4,32,128]{3,2,1,0:T(8,128)} copy(f32[5,4,32,128]{3,2,1,0:T(8,128)S(1)} %sweeps.1) | data formatting | bytes 655360

commit v4 on v3

--- a/solution.py
+++ b/solution.py
@@ -89,6 +89,7 @@
     spread_recv,
     last_recv,
     halo_recv,
+    present,
 ):
     row, span, pitch = lax.axis_index("row"), lax.axis_index("span"), lax.axis_index("pitch")
     length = 128 * pitches
@@ -107,11 +108,6 @@
         pl.semaphore_signal(barrier, inc=1, device_id=target, device_id_type=MESH)
 
     offsets = sorted(range(pitches), key=lambda o: -min(o, pitches - o))
-
-    def partners_of(there):
-        for o in offsets:
-            for half in (span, other):
-                greet({"row": there, "span": half, "pitch": lax.rem(pitch + o, pitches)})
 
     def donor_load(slot, where):
         cells = pl.ds(pl.multiple_of(where * 128, 128), 128)
@@ -137,19 +133,39 @@
     ):
         copy.start()
 
-    @pl.when(row > 0)
-    def _():
-        partners_of(row - 1)
-
-    @pl.when(row < last)
-    def _():
-        partners_of(row + 1)
+    for there, exists in ((row - 1, row > 0), (row + 1, row < last)):
+
+        @pl.when(exists)
+        def _():
+            greet({"row": there})
+            greet({"row": there, "span": other})
 
     greet({"span": other})
-    for o in range(1, pitches):
-        greet({"pitch": lax.rem(pitch + o, pitches)})
     for side in (right, left):
+        greet({"pitch": side})
         greet({"span": other, "pitch": side})
+
+    def tell(semaphore, target):
+        pl.semaphore_signal(semaphore, inc=1, device_id=target, device_id_type=MESH)
+
+    def tell_ring(i):
+        step = 1 + i
+        for o in (step, pitches - step):
+            tell(present.at[i], {"pitch": lax.rem(pitch + o, pitches)})
+
+    def hear_ring(i):
+        pl.semaphore_wait(present.at[i], 2)
+
+    def tell_downstream():
+        @pl.when(row < last)
+        def _():
+            tell(present.at[2], {"row": row + 1})
+            tell(present.at[2], {"row": row + 1, "span": other})
+
+    def hear_upstream():
+        @pl.when(row > 0)
+        def _():
+            pl.semaphore_wait(present.at[2], 2)
 
     def take(semaphore, tiles):
         there = gauge.at[0:tiles]
@@ -212,7 +228,7 @@
             src_ref=reduced.at[n],
             dst_ref=coef_in.at[n, landing],
             send_sem=sent.at[1 + beyond],
-            recv_sem=spread_recv.at[n],
+            recv_sem=spread_recv.at[n, beyond],
             device_id={"row": upstream, "span": other if beyond else span, "pitch": target},
             device_id_type=MESH,
         )
@@ -233,10 +249,11 @@
                 for o in offsets:
                     spread_copy(n, 1, lax.rem(pitch + o, pitches)).start()
 
-    def wait_coefs(n):
+    def wait_coefs(n, parts=(0, 1)):
         @pl.when(row < last)
         def _():
-            take(spread_recv.at[n], 5)
+            for beyond in parts:
+                take(spread_recv.at[n, beyond], 1 if beyond else 4)
 
     def last_copy(target):
         return pltpu.make_async_remote_copy(
@@ -303,9 +320,15 @@
         ]
 
     side_halos = [side_copies(half) for half in (0, 1)]
-    start_halo = halo_copy(
-        2, buf.at[0, 0, :, :, edge, :], buf.at[0, 0, :, :, 32:40, :], {"span": other}
-    )
+    start_halos = [
+        halo_copy(
+            2 + 6 * half,
+            buf.at[0, 0, :, 2 * half : 2 * half + 2, edge, :],
+            buf.at[0, 0, :, 2 * half : 2 * half + 2, 32:40, :],
+            {"span": other},
+        )
+        for half in (0, 1)
+    ]
     layer_halos = [
         halo_copy(3 + a, cpl.at[0, :, a, near, :], cpl.at[0, :, a, far, :], {"span": other})
         for a in range(4)
@@ -386,6 +409,7 @@
 
     main = ((0, 0, 32),)
     full = ((0, 0, 40), (1, 0, 40))
+    rest = ((0, 32, 40), (1, 0, 40))
 
     def coefs_of(n, lo, hi):
         if n < ITERS - 1:
@@ -395,17 +419,30 @@
             coefs = coefs + last_in[o, lo:hi]
         return split(coefs)
 
-    def add_boundary(n, chunks):
+    def add_boundary(n, chunks, ahead=False):
         for tile, lo, hi in chunks:
             high, low = coefs_of(n, lo, hi)
             table = (slice(None), slice(640 * tile, 640 * tile + 640))
             field = dot(high, syn_hi[table]) + (dot(low, syn_hi[table]) + dot(high, syn_lo[table]))
+            shares = [
+                field[:, 128 * c : 128 * c + 128] * inv[tile, lo:hi] for c in range(5)
+            ]
             for c in range(5):
-                share = field[:, 128 * c : 128 * c + 128] * inv[tile, lo:hi]
                 if n == ITERS - 1:
-                    result[c, 3] = result[c, 3] + share
+                    result[c, 3] = result[c, 3] + shares[c]
                 else:
-                    buf[n + 1, tile, c, 3, lo:hi] = buf[n + 1, tile, c, 3, lo:hi] + share
+                    buf[n + 1, tile, c, 3, lo:hi] = buf[n + 1, tile, c, 3, lo:hi] + shares[c]
+            if ahead and (n < ITERS - 2 or tile == 0):
+                end = hi if n < ITERS - 2 else 32
+                for c in range(5):
+                    mixed = jac[0, c, 0, 0] * shares[0][: end - lo]
+                    for j in range(1, 5):
+                        mixed = mixed + jac[j, c, 0, 0] * shares[j][: end - lo]
+                    mixed = cpl[tile, 0, 2, lo:end] * mixed
+                    if n < ITERS - 2:
+                        buf[n + 2, tile, c, 2, lo:end] = buf[n + 2, tile, c, 2, lo:end] + mixed
+                    else:
+                        result[c, 2] = result[c, 2] + mixed
 
     for copy in loads[0:4]:
         copy.wait()
@@ -430,18 +467,15 @@
     pack()
 
     linked = (row > 0).astype(I32) + (row < last).astype(I32)
-    pl.semaphore_wait(barrier, 2 + pitches + 2 * pitches * linked)
-    for copy in side_halos[0]:
+    pl.semaphore_wait(barrier, 5 + 2 * linked)
+    tell_ring(0)
+    for copy in side_halos[0] + [start_halos[0], layer_halos[0], start_halos[1]]:
         copy.start()
-    start_halo.start()
-    layer_halos[0].start()
-    for copy in side_halos[1]:
+    for copy in side_halos[1] + layer_halos[1:] + [last_halo]:
         copy.start()
-    for copy in layer_halos[1:]:
-        copy.start()
-    last_halo.start()
     project(0)
-    send_coefs(0)
+    hear_ring(0)
+    tell_ring(1)
 
     loads[5].wait()
     loads[6].wait()
@@ -499,52 +533,65 @@
     def wait_scale():
         last_halo.wait_recv()
 
-    def wait_start():
-        start_halo.wait_recv()
-
-    reduce_coefs(0)
+    def wait_start(half):
+        start_halos[half].wait_recv()
+
+    hear_ring(1)
+    tell_downstream()
+    send_coefs(0)
     wait_sides(0)
     unpack(0)
     unpack(1)
-    wait_start()
+    wait_start(0)
     wait_layer(0)
-    sweep_layer(0, 0, full)
+    sweep_layer(0, 0, main)
     project(1)
     send_coefs(1)
+    sweep_layer(0, 0, rest)
+    hear_upstream()
+    reduce_coefs(0)
     wait_sides(1)
     unpack(2)
+    wait_start(1)
     wait_layer(1)
     sweep_layer(0, 1, full)
-    sweep_layer(1, 0, full)
+    sweep_layer(1, 0, main)
     project(2)
     send_coefs(2)
+    sweep_layer(1, 0, rest)
     unpack(3)
     wait_layer(2)
     sweep_layer(0, 2, full)
     sweep_layer(1, 1, full)
-    sweep_layer(2, 0, full)
+    sweep_layer(2, 0, main)
     project(3)
     send_coefs(3)
     reduce_coefs(1)
+    sweep_layer(2, 0, rest)
 
     unpack(4)
     wait_layer(3)
     wait_scale()
     sweep_layer(0, 3, full)
-    wait_coefs(0)
-    add_boundary(0, full)
     reduce_coefs(2)
-    sweep_layer(1, 2, full)
-    sweep_layer(2, 1, full)
-    sweep_layer(3, 0, full)
+    wait_coefs(0, (0,))
+    add_boundary(0, main)
+    sweep_layer(1, 2, main)
+    sweep_layer(2, 1, main)
+    sweep_layer(3, 0, main)
     project(4)
+    reduce_coefs(3)
     send_last()
+    wait_coefs(0, (1,))
+    add_boundary(0, rest)
+    sweep_layer(1, 2, rest)
+    sweep_layer(2, 1, rest)
+    sweep_layer(3, 0, rest)
 
     sweep_layer(1, 3, full)
-    reduce_coefs(3)
+    sweep_layer(2, 2, full)
     wait_coefs(1)
-    add_boundary(1, full)
-    sweep_layer(2, 2, full)
+    add_boundary(1, full, ahead=True)
     sweep_layer(2, 3, full)
     sweep_layer(3, 1, full)
     sweep_layer(4, 0, main)
@@ -553,9 +600,9 @@
     sweep_layer(3, 2, full)
     sweep_layer(4, 1, main)
     sweep_layer(3, 3, full)
+    sweep_layer(4, 2, main)
     wait_coefs(3)
-    add_boundary(3, full)
-    sweep_layer(4, 2, main)
+    add_boundary(3, full, ahead=True)
     sweep_layer(4, 3, main)
     wait_last()
     add_boundary(4, main)
@@ -619,9 +666,10 @@
         dma((9,)),
         dma((3,)),
         dma((ITERS - 1,)),
-        dma((ITERS - 1,)),
+        dma((ITERS - 1, 2)),
         dma((1,)),
-        dma((8,)),
+        dma((9,)),
+        pltpu.SemaphoreType.REGULAR((3,)),
     ]
 
     def body(*refs):

time: 32.7 us -> 31.6 us (0.966)
  Pallas kernels: 31.8 us -> 30.7 us
    pallas_call x1, Pallas kernels: 31.8 us -> 30.7 us  [on_device(): pl.pallas_call(body, name='sweeps', out_shape=pltpu.VMEM(adjoint_start.sh...]
where the time goes in v4:
time: 31.6 us; the launch traced here: 31.5 us
  Pallas kernels  30.7 us (97%)
  local copies, waits for them, and re-layouts  0.73 us (2%)
    pallas_call x1, Pallas kernels, on_device(): pl.pallas_call(body, name='sweeps', out_shape=pltpu.VMEM(adjoint_start.sh...  30.7 us
    unnamed x1, local copies, waits for them, and re-layouts  0.73 us

profile of v4, /device:TPU:1, one launch (start us, length us, event | category | flops | bytes accessed | tf_op | source)
XLA Modules:
  0.0 31.5 jit_solution(12614595155192046344)
XLA Ops:
  0.0 30.7 %sweeps.1 = f32[5,4,32,128]{3,2,1,0:T(8,128)S(1)} custom-call(f32[5,4,32,128]{3,2,1,0:T(8,128)} %refs_0_.1, f32[5,4,32,128]{3,2,1,0:T(8,128)} %refs_1_.1, f32[6,4,32,128]{3,2,1,0:T(8,128)} %refs_2_.1, f32[4,32,128]{2,1,0:T(8,128)} %refs_3_.1, f32[5,5,1,6]{3,2,1,0:T(1,128)} %bitcast.7, f32[5,5,15,64]{3,2,1,0:T(8,128)} %bitcast.4, f32[5,5,15,64]{3,2,1,0:T(8,128)} %bitcast.5, ...), custom_call_target="tpu_custom_call" | custom-call | tf_op jit(solution)/shard_map/sweeps/pallas_call | solution.py:678
  30.7 0.7 %copy.12 = f32[5,4,32,128]{3,2,1,0:T(8,128)} copy(f32[5,4,32,128]{3,2,1,0:T(8,128)S(1)} %sweeps.1) | data formatting | bytes 655360

commit v5 on v4

--- a/solution.py
+++ b/solution.py
@@ -144,28 +144,29 @@
     for side in (right, left):
         greet({"pitch": side})
         greet({"span": other, "pitch": side})
+    for o in (2, pitches - 2):
+        greet({"pitch": lax.rem(pitch + o, pitches)})
 
     def tell(semaphore, target):
         pl.semaphore_signal(semaphore, inc=1, device_id=target, device_id_type=MESH)
 
-    def tell_ring(i):
-        step = 1 + i
-        for o in (step, pitches - step):
-            tell(present.at[i], {"pitch": lax.rem(pitch + o, pitches)})
-
-    def hear_ring(i):
-        pl.semaphore_wait(present.at[i], 2)
+    def tell_ring():
+        for o in (2, pitches - 2):
+            tell(present.at[0], {"pitch": lax.rem(pitch + o, pitches)})
+
+    def hear_ring():
+        pl.semaphore_wait(present.at[0], 2)
 
     def tell_downstream():
         @pl.when(row < last)
         def _():
-            tell(present.at[2], {"row": row + 1})
-            tell(present.at[2], {"row": row + 1, "span": other})
+            tell(present.at[1], {"row": row + 1})
+            tell(present.at[1], {"row": row + 1, "span": other})
 
     def hear_upstream():
         @pl.when(row > 0)
         def _():
-            pl.semaphore_wait(present.at[2], 2)
+            pl.semaphore_wait(present.at[1], 2)
 
     def take(semaphore, tiles):
         there = gauge.at[0:tiles]
@@ -467,15 +468,16 @@
     pack()
 
     linked = (row > 0).astype(I32) + (row < last).astype(I32)
-    pl.semaphore_wait(barrier, 5 + 2 * linked)
-    tell_ring(0)
+    pl.semaphore_wait(barrier, 7 + 2 * linked)
+    tell_ring()
     for copy in side_halos[0] + [start_halos[0], layer_halos[0], start_halos[1]]:
         copy.start()
     for copy in side_halos[1] + layer_halos[1:] + [last_halo]:
         copy.start()
     project(0)
-    hear_ring(0)
-    tell_ring(1)
+    hear_ring()
+    tell_downstream()
+    send_coefs(0)
 
     loads[5].wait()
     loads[6].wait()
@@ -536,9 +538,6 @@
     def wait_start(half):
         start_halos[half].wait_recv()
 
-    hear_ring(1)
-    tell_downstream()
-    send_coefs(0)
     wait_sides(0)
     unpack(0)
     unpack(1)
@@ -547,9 +546,9 @@
     sweep_layer(0, 0, main)
     project(1)
     send_coefs(1)
-    sweep_layer(0, 0, rest)
     hear_upstream()
     reduce_coefs(0)
+    sweep_layer(0, 0, rest)
     wait_sides(1)
     unpack(2)
     wait_start(1)
@@ -669,7 +668,7 @@
         dma((ITERS - 1, 2)),
         dma((1,)),
         dma((9,)),
-        pltpu.SemaphoreType.REGULAR((3,)),
+        pltpu.SemaphoreType.REGULAR((2,)),
     ]
 
     def body(*refs):

time: 31.6 us -> 30.4 us (0.962)
  Pallas kernels: 30.7 us -> 29.6 us
    pallas_call x1, Pallas kernels: 30.7 us -> 29.6 us  [on_device(): pl.pallas_call(body, name='sweeps', out_shape=pltpu.VMEM(adjoint_start.sh...]
where the time goes in v5:
time: 30.4 us
  Pallas kernels  29.6 us (97%)
  local copies, waits for them, and re-layouts  0.73 us (2%)
    pallas_call x1, Pallas kernels, on_device(): pl.pallas_call(body, name='sweeps', out_shape=pltpu.VMEM(adjoint_start.sh...  29.6 us
    unnamed x1, local copies, waits for them, and re-layouts  0.73 us

profile of v5, /device:TPU:1, one launch (start us, length us, event | category | flops | bytes accessed | tf_op | source)
XLA Modules:
  0.0 30.4 jit_solution(7093800508233884399)
XLA Ops:
  0.0 29.6 %sweeps.1 = f32[5,4,32,128]{3,2,1,0:T(8,128)S(1)} custom-call(f32[5,4,32,128]{3,2,1,0:T(8,128)} %refs_0_.1, f32[5,4,32,128]{3,2,1,0:T(8,128)} %refs_1_.1, f32[6,4,32,128]{3,2,1,0:T(8,128)} %refs_2_.1, f32[4,32,128]{2,1,0:T(8,128)} %refs_3_.1, f32[5,5,1,6]{3,2,1,0:T(1,128)} %bitcast.7, f32[5,5,15,64]{3,2,1,0:T(8,128)} %bitcast.4, f32[5,5,15,64]{3,2,1,0:T(8,128)} %bitcast.5, ...), custom_call_target="tpu_custom_call" | custom-call | tf_op jit(solution)/shard_map/sweeps/pallas_call | solution.py:677
  29.6 0.7 %copy.12 = f32[5,4,32,128]{3,2,1,0:T(8,128)} copy(f32[5,4,32,128]{3,2,1,0:T(8,128)S(1)} %sweeps.1) | data formatting | bytes 655360

commit v6 on v5

--- a/solution.py
+++ b/solution.py
@@ -420,7 +420,7 @@
             coefs = coefs + last_in[o, lo:hi]
         return split(coefs)
 
-    def add_boundary(n, chunks, ahead=False):
+    def add_boundary(n, chunks, ahead=0):
         for tile, lo, hi in chunks:
             high, low = coefs_of(n, lo, hi)
             table = (slice(None), slice(640 * tile, 640 * tile + 640))
@@ -433,17 +433,25 @@
                     result[c, 3] = result[c, 3] + shares[c]
                 else:
                     buf[n + 1, tile, c, 3, lo:hi] = buf[n + 1, tile, c, 3, lo:hi] + shares[c]
-            if ahead and (n < ITERS - 2 or tile == 0):
-                end = hi if n < ITERS - 2 else 32
+            if n == ITERS - 2 and tile:
+                continue
+            end = 32 if n == ITERS - 2 else hi
+            above = [share[: end - lo] for share in shares]
+            for depth in range(1, ahead + 1):
+                layer, then = 3 - depth, n + 1 + depth
+                passed = []
                 for c in range(5):
-                    mixed = jac[0, c, 0, 0] * shares[0][: end - lo]
+                    mixed = jac[0, c, 0, 0] * above[0]
                     for j in range(1, 5):
-                        mixed = mixed + jac[j, c, 0, 0] * shares[j][: end - lo]
-                    mixed = cpl[tile, 0, 2, lo:end] * mixed
-                    if n < ITERS - 2:
-                        buf[n + 2, tile, c, 2, lo:end] = buf[n + 2, tile, c, 2, lo:end] + mixed
+                        mixed = mixed + jac[j, c, 0, 0] * above[j]
+                    passed.append(cpl[tile, 0, layer, lo:end] * mixed)
+                above = passed
+                for c in range(5):
+                    if then == ITERS:
+                        result[c, layer] = result[c, layer] + above[c]
                     else:
-                        result[c, 2] = result[c, 2] + mixed
+                        old = buf[then, tile, c, layer, lo:end]
+                        buf[then, tile, c, layer, lo:end] = old + above[c]
 
     for copy in loads[0:4]:
         copy.wait()
@@ -572,12 +580,12 @@
     wait_layer(3)
     wait_scale()
     sweep_layer(0, 3, full)
+    sweep_layer(1, 2, main)
     reduce_coefs(2)
-    wait_coefs(0, (0,))
-    add_boundary(0, main)
-    sweep_layer(1, 2, main)
     sweep_layer(2, 1, main)
     sweep_layer(3, 0, main)
+    wait_coefs(0, (0,))
+    add_boundary(0, main, ahead=3)
     project(4)
     reduce_coefs(3)
     send_last()
@@ -590,7 +598,7 @@
     sweep_layer(1, 3, full)
     sweep_layer(2, 2, full)
     wait_coefs(1)
-    add_boundary(1, full, ahead=True)
+    add_boundary(1, full, ahead=1)
     sweep_layer(2, 3, full)
     sweep_layer(3, 1, full)
     sweep_layer(4, 0, main)
@@ -601,7 +609,7 @@
     sweep_layer(3, 3, full)
     sweep_layer(4, 2, main)
     wait_coefs(3)
-    add_boundary(3, full, ahead=True)
+    add_boundary(3, full, ahead=1)
     sweep_layer(4, 3, main)
     wait_last()
     add_boundary(4, main)

time: 30.4 us -> 30.1 us (level)
    pallas_call x1, Pallas kernels: 29.6 us -> 29.3 us  [on_device(): pl.pallas_call(body, name='sweeps', out_shape=pltpu.VMEM(adjoint_start.sh...]
where the time goes in v6:
time: 30.1 us; the launch traced here: 30 us
  Pallas kernels  29.3 us (97%)
  local copies, waits for them, and re-layouts  0.73 us (2%)
    pallas_call x1, Pallas kernels, on_device(): pl.pallas_call(body, name='sweeps', out_shape=pltpu.VMEM(adjoint_start.sh...  29.3 us
    unnamed x1, local copies, waits for them, and re-layouts  0.73 us

profile of v6, /device:TPU:1, one launch (start us, length us, event | category | flops | bytes accessed | tf_op | source)
XLA Modules:
  0.0 30.0 jit_solution(17490092269640811284)
XLA Ops:
  0.0 29.3 %sweeps.1 = f32[5,4,32,128]{3,2,1,0:T(8,128)S(1)} custom-call(f32[5,4,32,128]{3,2,1,0:T(8,128)} %refs_0_.1, f32[5,4,32,128]{3,2,1,0:T(8,128)} %refs_1_.1, f32[6,4,32,128]{3,2,1,0:T(8,128)} %refs_2_.1, f32[4,32,128]{2,1,0:T(8,128)} %refs_3_.1, f32[5,5,1,6]{3,2,1,0:T(1,128)} %bitcast.7, f32[5,5,15,64]{3,2,1,0:T(8,128)} %bitcast.4, f32[5,5,15,64]{3,2,1,0:T(8,128)} %bitcast.5, ...), custom_call_target="tpu_custom_call" | custom-call | tf_op jit(solution)/shard_map/sweeps/pallas_call | solution.py:685
  29.3 0.7 %copy.12 = f32[5,4,32,128]{3,2,1,0:T(8,128)} copy(f32[5,4,32,128]{3,2,1,0:T(8,128)S(1)} %sweeps.1) | data formatting | bytes 655360
